TPU v7x, 128 devices: a whole 4x4x4 slice. The times are simulated.
128 devices in a mesh: tm: 16 (over z, y), height: 8 (over x, core).
Axes of the slice: x: 4, y: 4, z: 4, core: 2. Of those that a mesh axis runs over, the one named last changes fastest.
Arguments:
- latents: bfloat16 [32, 32, 128, 256], P('tm', 'height'), may hold values from -6 to 6
- conv_first: bfloat16 [3, 3, 3, 256, 256], replicated, may hold values from -0.078125 to 0.078125
- conv_second: bfloat16 [3, 3, 3, 256, 256], replicated, may hold values from -0.078125 to 0.078125
- codebook: bfloat16 [262144, 256], P('height'), may hold values from -13 to 13
- codes: int32 [32, 32, 128], P('tm', 'height'), may hold values from 0 to 262143, as said below
- upstream: bfloat16 [32, 32, 128, 256], P('tm', 'height'), may hold values from -6 to 6
Outputs:
- grad_latent: bfloat16 [32, 32, 128, 256], P('tm', 'height')
- codebook_grad: bfloat16 [262144, 256], P(('height', 'tm'))
Inputs may be any that keep to these rules, and one draw needn't show every extreme that they name: Each device's 1024 cells hold at most 16 codes of any one aligned range of 2048 codes; some ranges receive exactly 16 from every device.
All inputs are finite; a program needn't handle non-finite values.
Results may differ from a plain program's by a relative error of at most 0.0085.
Values may be sent and summed in bfloat16 or wider, within the bound.
A program may use at most 128 MiB of HBM per device.

v0:
```python
import jax
import jax.numpy as jnp
from jax import lax
from jax.sharding import PartitionSpec as P

COMMIT = 0.25


def passed_along(x, axis, by):
    count = lax.axis_size(axis)
    pairs = [(i, i + by) for i in range(count) if 0 <= i + by < count]
    return lax.ppermute(x, axis, pairs)


def extended_2(block, sides, width):
    for axis, dim in sides:
        count = lax.axis_size(axis)
        forward = [(i, i + 1) for i in range(count - 1)]
        backward = [(target, source) for source, target in forward]
        low = lax.ppermute(
            lax.slice_in_dim(block, block.shape[dim] - width, None, axis=dim), axis, forward
        )
        high = lax.ppermute(lax.slice_in_dim(block, 0, width, axis=dim), axis, backward)
        block = jnp.concatenate([low, block, high], axis=dim)
    return block


def norm_act(video):
    values = video.astype(jnp.float32)
    scaled = values * lax.rsqrt(jnp.mean(values * values, -1, keepdims=True) + 1e-06)
    return jax.nn.silu(scaled).astype(jnp.bfloat16)


def conv_block(video, weight):
    frames, rows, columns, channels = video.shape
    active = norm_act(video)
    earlier = passed_along(active, "tm", 1)
    extended = jnp.concatenate([earlier, active], 0)
    extended = extended_2(extended, (("height", 1),), 1)
    extended = jnp.pad(extended, ((0, 0), (0, 0), (1, 1), (0, 0)))
    pieces = [
        extended[step_t : step_t + frames, step_h : step_h + rows, step_w : step_w + columns, :]
        for step_t in range(3)
        for step_h in range(3)
        for step_w in range(3)
    ]
    patch = jnp.concatenate(pieces, -1).reshape(frames * rows * columns, 27 * channels)
    conv = jnp.dot(
        patch, weight.reshape(27 * channels, channels), preferred_element_type=jnp.float32
    )
    return (video.astype(jnp.float32) + conv.reshape(video.shape)).astype(jnp.bfloat16)


def rotate_back(latent, quant, upward):
    lat_norm = jnp.sqrt(jnp.sum(latent * latent, -1, keepdims=True) + 1e-06)
    quant_norm = jnp.sqrt(jnp.sum(quant * quant, -1, keepdims=True) + 1e-06)
    lat_unit = latent / lat_norm
    quant_unit = quant / quant_norm
    cosine = jnp.sum(lat_unit * quant_unit, -1, keepdims=True)
    summed = lat_unit + quant_unit
    turned = upward - summed * (jnp.sum(summed * upward, -1, keepdims=True) / (1.0 + cosine))
    turned = turned + 2.0 * lat_unit * jnp.sum(quant_unit * upward, -1, keepdims=True)
    return quant_norm / lat_norm * turned + 2.0 * COMMIT * (latent - quant)


def on_device(latents, conv_first, conv_second, codebook, codes, upstream):
    first = conv_block(latents, conv_first)
    encoded = conv_block(first, conv_second)
    frames, rows, columns, channels = encoded.shape
    cells = frames * rows * columns
    latent_flat = encoded.reshape(cells, channels).astype(jnp.float32)
    code_flat = codes.reshape(cells)
    rows_held = codebook.shape[0]
    shard_base = lax.axis_index("height") * rows_held
    tiles = lax.axis_size("tm")
    groups = lax.axis_size("height")
    owners = tiles * groups
    range_rows = rows_held // tiles
    capacity = 2 * cells // owners
    block_id = code_flat // range_rows
    target_dev = block_id % tiles * groups + block_id // tiles
    hits = (target_dev[:, None] == jnp.arange(owners, dtype=jnp.int32)[None, :]).astype(jnp.int32)
    place_rank = jnp.sum(jnp.cumsum(hits, 0) * hits, 1) - 1
    slot_index = target_dev * capacity + place_rank
    slot_codes = jnp.full((owners * capacity,), -1, jnp.int32).at[slot_index].set(code_flat)
    owner_codes = lax.all_to_all(
        slot_codes.reshape(owners, capacity),
        ("tm", "height"),
        split_axis=0,
        concat_axis=0,
        tiled=True,
    )
    present = owner_codes >= 0
    local_rows = jnp.clip(owner_codes - shard_base, 0, rows_held - 1)
    found_rows = jnp.take(codebook, local_rows, axis=0)
    found_rows = jnp.where(present[..., None], found_rows, jnp.zeros_like(found_rows))
    rows_back = lax.all_to_all(
        found_rows, ("tm", "height"), split_axis=0, concat_axis=0, tiled=True
    )
    quant = jnp.take(rows_back.reshape(owners * capacity, channels), slot_index, axis=0).astype(
        jnp.float32
    )
    upward = upstream.reshape(cells, channels).astype(jnp.float32)
    grad_flat = rotate_back(latent_flat, quant, upward)
    diff = (quant - latent_flat).astype(jnp.bfloat16)
    term_slots = jnp.zeros((owners * capacity, channels), jnp.bfloat16).at[slot_index].set(diff)
    owner_terms = lax.all_to_all(
        term_slots.reshape(owners, capacity, channels),
        ("tm", "height"),
        split_axis=0,
        concat_axis=0,
        tiled=True,
    )
    tile_base = shard_base + lax.axis_index("tm") * range_rows
    target_rows = jnp.where(present, owner_codes - tile_base, range_rows)
    sums = (
        jnp.zeros((range_rows, channels), jnp.float32)
        .at[target_rows.reshape(-1)]
        .add(owner_terms.reshape(-1, channels).astype(jnp.float32), mode="drop")
    )
    grad_latent = grad_flat.astype(jnp.bfloat16).reshape(upstream.shape)
    return (grad_latent, (2.0 * sums).astype(jnp.bfloat16))


def solution(mesh):
    return jax.shard_map(
        on_device,
        mesh=mesh,
        in_specs=(
            P("tm", "height", None, None),
            P(),
            P(),
            P("height", None),
            P("tm", "height", None),
            P("tm", "height", None, None),
        ),
        out_specs=(P("tm", "height", None, None), P(("height", "tm"), None)),
        check_vma=False,
    )
```

profile of v0, /device:TPU:1, one launch (start us, length us, event | category | flops | bytes accessed | tf_op | source)
XLA Modules:
  0.0 182.7 jit_solution(14054549658392838709)
XLA Ops:
  2.7 2.2 %fusion.20 = bf16[2,4,128,256]{3,2,1,0:T(8,128)(2,1)} fusion(bf16[2,4,128,256]{3,2,1,0:T(8,128)(2,1)} %param.6, f32[2,4,128]{2,1,0:T(4,128)S(1)} %add_rsqrt_fusion.1), kind=kLoop, calls=%fused_computation.50 | loop fusion | flops 1835008 | bytes 1052672 | tf_op jit(solution)/shard_map/convert_element_type | solution.py:31
  4.8 4.8 %collective-permute-start = (bf16[2,4,128,256]{3,2,1,0:T(8,128)(2,1)}, bf16[2,4,128,256]{3,2,1,0:T(8,128)(2,1)}, u32[]{:S(2)}, u32[]{:S(2)}) collective-permute-start(bf16[2,4,128,256]{3,2,1,0:T(8,128)(2,1)} %fusion.20), channel_id=1, source_target_pairs={{0,8},{8,16},{16,24},{24,32},{32,40},{40,48},{48,56},{56,64},{64,7... | collective-permute-start | bytes 1572872 | tf_op jit(solution)/shard_map/ppermute | solution.py:12
  16.6 4.5 %scatter_custom_fusion = s32[2048]{0:T(1024)S(1)} fusion(s32[1024]{0:T(1024)S(1)} %bitcast.67, s32[1024]{0:T(1024)} %bitcast.60, s32[]{:T(128)} %constant.101.clone.1), kind=kCustom, calls=%fused_computation.209 | custom fusion | bytes 8704 | tf_op jit(solution)/shard_map/scatter | solution.py:85
  21.8 10.3 %all-to-all-start = ((s32[128,1,16]{2,1,0:T(1,128)}), s32[128,1,16]{2,1,0:T(1,128)}, u32[]{:S(2)}, u32[]{:S(2)}) async-start(s32[128,1,16]{2,1,0:T(1,128)} %bitcast.56), calls=%async_computation | async-start | bytes 131072 | tf_op jit(solution)/shard_map/all_to_all | solution.py:86
  33.4 8.0 %all-to-all-done = s32[128,1,16]{2,1,0:T(1,128)} async-done(((s32[128,1,16]{2,1,0:T(1,128)}), s32[128,1,16]{2,1,0:T(1,128)}, u32[]{:S(2)}, u32[]{:S(2)}) %all-to-all-start) | async-done | bytes 8224 | tf_op jit(solution)/shard_map/all_to_all | solution.py:86
  48.0 16.4 %gather_fusion = bf16[2048,256]{1,0:T(8,128)(2,1)} fusion(bf16[32768,256]{1,0:T(8,128)(2,1)} %param.9, s32[2048]{0:T(1024)S(1)} %broadcast_clamp_fusion), kind=kCustom, calls=%fused_computation | custom fusion | bytes 2105344 | tf_op jit(solution)/shard_map/jit(_take)/gather | solution.py:95
  66.4 3.1 %collective-permute-start.1 = (bf16[4,1,128,256]{3,2,1,0:T(8,128)(2,1)}, bf16[4,1,128,256]{3,2,1,0:T(8,128)(2,1)}, u32[]{:S(2)}, u32[]{:S(2)}) collective-permute-start(bf16[4,1,128,256]{3,2,1,0:T(8,128)(2,1)} %get-tuple-element.11), channel_id=1, source_target_pairs={{0,1},{1,2},{2,3},{3,4},{4,5},{5,6},{6,7},{8,9},{9,10},{10,11},{11... | collective-permute-start | bytes 786440 | tf_op jit(solution)/shard_map/ppermute | solution.py:20
  71.5 3.4 %select_select_fusion = bf16[128,16,256]{2,1,0:T(8,128)(2,1)} fusion(bf16[128,16,256]{2,1,0:T(8,128)(2,1)} %bitcast.54, pred[128,16]{1,0:T(8,128)(4,1)} %copy.20, pred[128,16]{1,0:T(8,128)(4,1)} %copy.18), kind=kLoop, calls=%fused_computation.65 | loop fusion | flops 1048576 | bytes 2101248 | tf_op jit(solution)/shard_map/jit(_where)/select_n | solution.py:96
  74.8 5.6 %all-to-all-start.1 = ((bf16[128,16,256]{2,1,0:T(8,128)(2,1)}), bf16[128,16,256]{2,1,0:T(8,128)(2,1)}, u32[]{:S(2)}, u32[]{:S(2)}) async-start(bf16[128,16,256]{2,1,0:T(8,128)(2,1)} %select_select_fusion), calls=%async_computation.1 | async-start | bytes 2097152 | tf_op jit(solution)/shard_map/all_to_all | solution.py:97
  80.4 2.2 %select_maximum_fusion.3 = bf16[4,6,130,256]{3,2,1,0:T(8,128)(2,1)S(1)} fusion(bf16[4,1,128,256]{3,2,1,0:T(8,128)(2,1)} %collective-permute-done.2, bf16[4,1,128,256]{3,2,1,0:T(8,128)(2,1)} %collective-permute-done.1, bf16[2,4,128,256]{3,2,1,0:T(8,128)(2,1)} %fusion.20, bf16[2,4,128,256]{3,2,1,0:T(8,128)(2,1)} %collective-permute-done), kind=kLoop, calls=%fused_computation.14 | loop fusion | flops 11980800 | bytes 3170304 | tf_op jit(solution)/shard_map/concatenate | solution.py:24
  89.2 3.9 %fusion.27 = (f32[2,4,128]{2,1,0:T(4,128)S(1)}, bf16[2,4,128,256]{3,2,1,0:T(8,128)(2,1)S(1)}) fusion(bf16[2,4,128,6912]{3,2,1,0:T(8,128)(2,1)S(1)} %slice_dynamic-update-slice_fusion.24, bf16[6912,256,1,1]{1,0,3,2:T(8,128)(2,1)S(1)} %bitcast.52, bf16[2,4,128,256]{3,2,1,0:T(8,128)(2,1)S(1)} %copy-done.4), kind=kOutput, calls=%fused_computation.57 | convolution fusion | flops 3625450496 | bytes 18747392 | tf_op jit(solution)/shard_map/dot_general | solution.py:48
  94.3 3.3 %collective-permute-start.3 = (bf16[2,4,128,256]{3,2,1,0:T(8,128)(2,1)S(1)}, bf16[2,4,128,256]{3,2,1,0:T(8,128)(2,1)S(1)}, u32[]{:S(2)}, u32[]{:S(2)}) collective-permute-start(bf16[2,4,128,256]{3,2,1,0:T(8,128)(2,1)S(1)} %fusion.16), channel_id=1, source_target_pairs={{0,8},{8,16},{16,24},{24,32},{32,40},{40,48},{48,56},{56,64},{64,7... | collective-permute-start | bytes 1572872 | tf_op jit(solution)/shard_map/ppermute | solution.py:12
  99.1 9.3 %collective-permute-done.3 = bf16[2,4,128,256]{3,2,1,0:T(8,128)(2,1)S(1)} collective-permute-done((bf16[2,4,128,256]{3,2,1,0:T(8,128)(2,1)S(1)}, bf16[2,4,128,256]{3,2,1,0:T(8,128)(2,1)S(1)}, u32[]{:S(2)}, u32[]{:S(2)}) %collective-permute-start.3) | collective-permute-done | bytes 524320 | tf_op jit(solution)/shard_map/ppermute | solution.py:12
  108.5 4.2 %collective-permute-start.4 = (bf16[4,1,128,256]{3,2,1,0:T(8,128)(2,1)S(1)}, bf16[4,1,128,256]{3,2,1,0:T(8,128)(2,1)S(1)}, u32[]{:S(2)}, u32[]{:S(2)}) collective-permute-start(bf16[4,1,128,256]{3,2,1,0:T(8,128)(2,1)S(1)} %get-tuple-element.7), channel_id=1, source_target_pairs={{0,1},{1,2},{2,3},{3,4},{4,5},{5,6},{6,7},{8,9},{9,10},{10,11},{11... | collective-permute-start | bytes 786440 | tf_op jit(solution)/shard_map/ppermute | solution.py:20
  112.7 2.1 %collective-permute-start.5 = (bf16[4,1,128,256]{3,2,1,0:T(8,128)(2,1)S(1)}, bf16[4,1,128,256]{3,2,1,0:T(8,128)(2,1)S(1)}, u32[]{:S(2)}, u32[]{:S(2)}) collective-permute-start(bf16[4,1,128,256]{3,2,1,0:T(8,128)(2,1)S(1)} %get-tuple-element.8), channel_id=1, source_target_pairs={{1,0},{2,1},{3,2},{4,3},{5,4},{6,5},{7,6},{9,8},{10,9},{11,10},{12... | collective-permute-start | bytes 786440 | tf_op jit(solution)/shard_map/ppermute | solution.py:23
  114.9 6.0 %gather_fusion.1 = bf16[1024,256]{1,0:T(8,128)(2,1)} fusion(bf16[2048,256]{1,0:T(8,128)(2,1)} %bitcast.13, s32[1024]{0:T(1024)S(1)} %broadcast_clamp_fusion.1), kind=kCustom, calls=%fused_computation.1 | custom fusion | bytes 1052672 | tf_op jit(solution)/shard_map/jit(_take)/gather | solution.py:100
  124.4 4.5 %multiply_reduce_fusion.1 = (f32[2,4,128]{2,1,0:T(4,128)}, f32[2,4,128,256]{3,2,1,0:T(8,128)S(1)}) fusion(bf16[2,4,128,6912]{3,2,1,0:T(8,128)(2,1)S(1)} %slice_dynamic-update-slice_fusion, bf16[6912,256,1,1]{1,0,3,2:T(8,128)(2,1)S(1)} %bitcast.71, bf16[2,4,128,256]{3,2,1,0:T(8,128)(2,1)S(1)} %copy-done.7), kind=kOutput, calls=%fused_computation.64 | convolution fusion | flops 3625450496 | bytes 19271680 | tf_op jit(solution)/shard_map/dot_general | solution.py:48
  130.9 6.4 %scatter_custom_fusion.1 = bf16[2048,256]{1,0:T(8,128)(2,1)} fusion(s32[1024]{0:T(1024)} %bitcast.68, bf16[1024,256]{1,0:T(8,128)(2,1)} %get-tuple-element.13, bf16[]{:T(256)} %constant.111.clone.1), kind=kCustom, calls=%fused_computation.120 | custom fusion | bytes 1049088 | tf_op jit(solution)/shard_map/scatter | solution.py:106
  137.3 11.4 %all-to-all-start.2 = ((bf16[128,16,256]{2,1,0:T(8,128)(2,1)}), bf16[128,16,256]{2,1,0:T(8,128)(2,1)}, u32[]{:S(2)}, u32[]{:S(2)}) async-start(bf16[128,16,256]{2,1,0:T(8,128)(2,1)} %bitcast.55), calls=%async_computation.2 | async-start | bytes 2097152 | tf_op jit(solution)/shard_map/all_to_all | solution.py:107
  149.4 2.3 %multiply_reduce_fusion = (f32[2,4,128]{2,1,0:T(4,128)S(1)}, f32[2,4,128]{2,1,0:T(4,128)S(1)}, f32[2,4,128]{2,1,0:T(4,128)S(1)}) fusion(f32[2,4,128,256]{3,2,1,0:T(8,128)} %copy-done.2, f32[2,4,128]{2,1,0:T(4,128)S(1)} %get-tuple-element.16, f32[2,4,128]{2,1,0:T(4,128)S(1)} %bitcast.63, bf16[2,4,128,256]{3,2,1,0:T(8,128)(2,1)} %bitcast.53, ...), kind=kLoop, calls=%fused_computation.63 | loop fusion | flops 3142656 | bytes 2118656 | tf_op jit(solution)/shard_map/reduce_sum | solution.py:59
  151.7 2.9 %fusion.25 = bf16[2,4,128,256]{3,2,1,0:T(8,128)(2,1)} fusion(f32[2,4,128,256]{3,2,1,0:T(8,128)} %copy-done.2, bf16[2,4,128,256]{3,2,1,0:T(8,128)(2,1)} %param.11, f32[2,4,128]{2,1,0:T(4,128)S(1)} %get-tuple-element.22, f32[2,4,128]{2,1,0:T(4,128)S(1)} %get-tuple-element.21, f32[2,4,128]{2,1,0:T(4,128)S(1)} %get-tuple-element.15, ...), kind=kLoop, calls=%fused_computation.55 | loop fusion | flops 3932160 | bytes 2642944 | tf_op jit(solution)/shard_map/convert_element_type | solution.py:121
  154.6 13.0 %all-to-all-done.2 = bf16[128,16,256]{2,1,0:T(8,128)(2,1)} async-done(((bf16[128,16,256]{2,1,0:T(8,128)(2,1)}), bf16[128,16,256]{2,1,0:T(8,128)(2,1)}, u32[]{:S(2)}, u32[]{:S(2)}) %all-to-all-start.2) | async-done | bytes 1048608 | tf_op jit(solution)/shard_map/all_to_all | solution.py:107
  167.6 12.4 %scatter_custom_fusion.2 = f32[2048,256]{1,0:T(8,128)} fusion(s32[2048]{0:T(1024)S(1)} %bitcast.70, bf16[2048,256]{1,0:T(8,128)(2,1)} %bitcast.32, f32[]{:T(128)} %constant.112.clone.1), kind=kCustom, calls=%fused_computation.8 | custom fusion | flops 1048576 | bytes 3145732 | tf_op jit(solution)/shard_map/scatter-add | solution.py:119
  179.9 2.7 %multiply_convert_fusion = bf16[2048,256]{1,0:T(8,128)(2,1)} fusion(f32[2048,256]{1,0:T(8,128)} %scatter_custom_fusion.2), kind=kLoop, calls=%fused_computation.10 | loop fusion | flops 1048576 | bytes 3145728 | tf_op jit(solution)/shard_map/convert_element_type | solution.py:122
  (137 shorter events, 36.3 us)
Async XLA Ops:
  0.6 88.5 %copy-start = (bf16[3,3,3,256,256]{4,3,2,1,0:T(8,128)(2,1)S(1)}, bf16[3,3,3,256,256]{4,3,2,1,0:T(8,128)(2,1)}, u32[]{:S(2)}) copy-start(bf16[3,3,3,256,256]{4,3,2,1,0:T(8,128)(2,1)} %param.7) | copy-start | bytes 10616836
  4.8 59.6 %collective-permute-start = (bf16[2,4,128,256]{3,2,1,0:T(8,128)(2,1)}, bf16[2,4,128,256]{3,2,1,0:T(8,128)(2,1)}, u32[]{:S(2)}, u32[]{:S(2)}) collective-permute-start(bf16[2,4,128,256]{3,2,1,0:T(8,128)(2,1)} %fusion.20), channel_id=1, source_target_pairs={{0,8},{8,16},{16,24},{24,32},{32,40},{40,48},{48,56},{56,64},{64,7... | collective-permute-start | bytes 1572872 | tf_op jit(solution)/shard_map/ppermute | solution.py:12
  12.1 0.8 copy-start.5
  16.6 16.8 %copy-start.12 = (s32[1024,1]{0,1:T(1,128)}, s32[1024,1]{0,1:T(1,128)S(1)}, u32[]{:S(2)}) copy-start(s32[1024,1]{0,1:T(1,128)S(1)} %compare_select_fusion.1) | copy-start | bytes 12292
  21.8 19.7 %all-to-all-start = ((s32[128,1,16]{2,1,0:T(1,128)}), s32[128,1,16]{2,1,0:T(1,128)}, u32[]{:S(2)}, u32[]{:S(2)}) async-start(s32[128,1,16]{2,1,0:T(1,128)} %bitcast.56), calls=%async_computation | async-start | bytes 131072 | tf_op jit(solution)/shard_map/all_to_all | solution.py:86
  66.4 14.0 %collective-permute-start.1 = (bf16[4,1,128,256]{3,2,1,0:T(8,128)(2,1)}, bf16[4,1,128,256]{3,2,1,0:T(8,128)(2,1)}, u32[]{:S(2)}, u32[]{:S(2)}) collective-permute-start(bf16[4,1,128,256]{3,2,1,0:T(8,128)(2,1)} %get-tuple-element.11), channel_id=1, source_target_pairs={{0,1},{1,2},{2,3},{3,4},{4,5},{5,6},{6,7},{8,9},{9,10},{10,11},{11... | collective-permute-start | bytes 786440 | tf_op jit(solution)/shard_map/ppermute | solution.py:20
  69.5 10.9 %collective-permute-start.2 = (bf16[4,1,128,256]{3,2,1,0:T(8,128)(2,1)}, bf16[4,1,128,256]{3,2,1,0:T(8,128)(2,1)}, u32[]{:S(2)}, u32[]{:S(2)}) collective-permute-start(bf16[4,1,128,256]{3,2,1,0:T(8,128)(2,1)} %get-tuple-element.12), channel_id=1, source_target_pairs={{1,0},{2,1},{3,2},{4,3},{5,4},{6,5},{7,6},{9,8},{10,9},{11,10},{12... | collective-permute-start | bytes 786440 | tf_op jit(solution)/shard_map/ppermute | solution.py:23
  74.8 40.0 %all-to-all-start.1 = ((bf16[128,16,256]{2,1,0:T(8,128)(2,1)}), bf16[128,16,256]{2,1,0:T(8,128)(2,1)}, u32[]{:S(2)}, u32[]{:S(2)}) async-start(bf16[128,16,256]{2,1,0:T(8,128)(2,1)} %select_select_fusion), calls=%async_computation.1 | async-start | bytes 2097152 | tf_op jit(solution)/shard_map/all_to_all | solution.py:97
  82.6 5.8 %copy-start.4 = (bf16[2,4,128,256]{3,2,1,0:T(8,128)(2,1)S(1)}, bf16[2,4,128,256]{3,2,1,0:T(8,128)(2,1)}, u32[]{:S(2)}) copy-start(bf16[2,4,128,256]{3,2,1,0:T(8,128)(2,1)} %param.6) | copy-start | bytes 1572868
  82.6 5.8 %copy-start.10 = (f32[2,4,128]{2,1,0:T(4,128)S(1)}, f32[2,4,128]{2,1,0:T(4,128)}, u32[]{:S(2)}) copy-start(f32[2,4,128]{2,1,0:T(4,128)} %copy-done.9) | copy-start | bytes 12292
  89.2 8.4 %copy-start.13 = (s32[1024,1]{0,1:T(1,128)S(1)}, s32[1024,1]{0,1:T(1,128)}, u32[]{:S(2)}) copy-start(s32[1024,1]{0,1:T(1,128)} %copy-done.12) | copy-start | bytes 12292
  89.2 8.4 %copy-start.8 = (s32[2,4,128]{2,1,0:T(4,128)S(1)}, s32[2,4,128]{2,1,0:T(4,128)}, u32[]{:S(2)}) copy-start(s32[2,4,128]{2,1,0:T(4,128)} %param.10) | copy-start | bytes 12292
  93.1 0.8 copy-start.6
  94.3 14.1 %collective-permute-start.3 = (bf16[2,4,128,256]{3,2,1,0:T(8,128)(2,1)S(1)}, bf16[2,4,128,256]{3,2,1,0:T(8,128)(2,1)S(1)}, u32[]{:S(2)}, u32[]{:S(2)}) collective-permute-start(bf16[2,4,128,256]{3,2,1,0:T(8,128)(2,1)S(1)} %fusion.16), channel_id=1, source_target_pairs={{0,8},{8,16},{16,24},{24,32},{32,40},{40,48},{48,56},{56,64},{64,7... | collective-permute-start | bytes 1572872 | tf_op jit(solution)/shard_map/ppermute | solution.py:12
  108.5 12.4 %collective-permute-start.4 = (bf16[4,1,128,256]{3,2,1,0:T(8,128)(2,1)S(1)}, bf16[4,1,128,256]{3,2,1,0:T(8,128)(2,1)S(1)}, u32[]{:S(2)}, u32[]{:S(2)}) collective-permute-start(bf16[4,1,128,256]{3,2,1,0:T(8,128)(2,1)S(1)} %get-tuple-element.7), channel_id=1, source_target_pairs={{0,1},{1,2},{2,3},{3,4},{4,5},{5,6},{6,7},{8,9},{9,10},{10,11},{11... | collective-permute-start | bytes 786440 | tf_op jit(solution)/shard_map/ppermute | solution.py:20
  112.7 8.1 %collective-permute-start.5 = (bf16[4,1,128,256]{3,2,1,0:T(8,128)(2,1)S(1)}, bf16[4,1,128,256]{3,2,1,0:T(8,128)(2,1)S(1)}, u32[]{:S(2)}, u32[]{:S(2)}) collective-permute-start(bf16[4,1,128,256]{3,2,1,0:T(8,128)(2,1)S(1)} %get-tuple-element.8), channel_id=1, source_target_pairs={{1,0},{2,1},{3,2},{4,3},{5,4},{6,5},{7,6},{9,8},{10,9},{11,10},{12... | collective-permute-start | bytes 786440 | tf_op jit(solution)/shard_map/ppermute | solution.py:23
  121.8 1.8 copy-start.7
  122.1 2.3 %copy-start.16 = (bf16[3,3,3,256,256]{4,3,2,1,0:T(8,128)(2,1)S(1)}, bf16[3,3,3,256,256]{4,3,2,1,0:T(8,128)(2,1)}, u32[]{:S(2)}) copy-start(bf16[3,3,3,256,256]{4,3,2,1,0:T(8,128)(2,1)} %param.8) | copy-start | bytes 10616836
  124.2 5.6 %copy-start.3 = (bf16[1024,256]{1,0:T(8,128)(2,1)S(1)}, bf16[1024,256]{1,0:T(8,128)(2,1)}, u32[]{:S(2)}) copy-start(bf16[1024,256]{1,0:T(8,128)(2,1)} %gather_fusion.1) | copy-start | bytes 1572868
  124.2 5.6 %copy-start.15 = (pred[1024]{0:T(1024)(128)(4,1)S(1)}, pred[1024]{0:T(1024)(128)(4,1)}, u32[]{:S(2)}) copy-start(pred[1024]{0:T(1024)(128)(4,1)} %compare_and_fusion.2) | copy-start | bytes 3076
  124.4 25.0 %copy-start.14 = (pred[2,4,128]{2,1,0:T(4,128)(4,1)S(1)}, pred[2,4,128]{2,1,0:T(4,128)(4,1)}, u32[]{:S(2)}) copy-start(pred[2,4,128]{2,1,0:T(4,128)(4,1)} %compare_and_fusion.1) | copy-start | bytes 3076
  124.4 58.3 %copy-start.1 = (bf16[3,3,3,256,256]{4,3,2,1,0:T(8,128)(2,1)S(1)}, bf16[3,3,3,256,256]{4,3,2,1,0:T(8,128)(2,1)}, u32[]{:S(2)}) copy-start(bf16[3,3,3,256,256]{4,3,2,1,0:T(8,128)(2,1)} %param.7) | copy-start | bytes 10616836
  128.9 1.0 copy-start.2
  137.3 30.2 %all-to-all-start.2 = ((bf16[128,16,256]{2,1,0:T(8,128)(2,1)}), bf16[128,16,256]{2,1,0:T(8,128)(2,1)}, u32[]{:S(2)}, u32[]{:S(2)}) async-start(bf16[128,16,256]{2,1,0:T(8,128)(2,1)} %bitcast.55), calls=%async_computation.2 | async-start | bytes 2097152 | tf_op jit(solution)/shard_map/all_to_all | solution.py:107
  (2 other events, 1.2 us)
where the time goes:
time: 184 us; the launch traced here: 183 us
  local copies, waits for them, and re-layouts  48.5 us (26%)
  other arithmetic  47.2 us (26%)
  starting transfers between devices  46.8 us (25%)
  waiting for transfers between devices  30.3 us (16%)
  matrix products  8.41 us (5%)
    gather x1, local copies, waits for them, and re-layouts, on_device(): found_rows = jnp.take(codebook, local_rows, axis=0)  16.4 us
    all_to_all x1, waiting for transfers between devices, on_device(): lax.all_to_all(term_slots.reshape(owners, capacity, channels), ('tm', 'he...  13 us
    scatter-add x1, other arithmetic, on_device(): sums = jnp.zeros((range_rows, channels), jnp.float32).at[target_rows.resh...  12.4 us
    all_to_all x1, starting transfers between devices, on_device(): lax.all_to_all(term_slots.reshape(owners, capacity, channels), ('tm', 'he...  11.4 us
    all_to_all x1, starting transfers between devices, on_device(): lax.all_to_all(slot_codes.reshape(owners, capacity), ('tm', 'height'), sp...  10.3 us
    ppermute x2, waiting for transfers between devices, passed_along(): return lax.ppermute(x, axis, pairs)  9.3 us
    dot_general x2, matrix products, conv_block(): jnp.dot(patch, weight.reshape(27 * channels, channels), preferred_element...  8.41 us
    ppermute x2, starting transfers between devices, passed_along(): return lax.ppermute(x, axis, pairs)  8.11 us
  transfers between devices with their start and end apart: 9, of which 3 were waited for; matrix products, arithmetic and copies ran while one was open for 35% of the time, Pallas kernels for 0%

commit v1 on v0

v1 whole, which is shorter than its diff:
```python
import functools

import jax
import jax.numpy as jnp
from jax import lax
from jax.experimental import pallas as pl
from jax.experimental.pallas import tpu as pltpu
from jax.sharding import PartitionSpec as P

F32 = jnp.float32
BF16 = jnp.bfloat16
I32 = jnp.int32
MESH = pl.DeviceIdType.MESH
C = 256
NT, NH = 16, 8
OWN = NT * NH
CAP = 16
SLOTS = OWN * CAP
K_OWN = 2048
CELLS = 1024
VMEM_LIMIT = 60 * 1024 * 1024


def onehot(cond):
    return jnp.where(cond, 1.0, 0.0).astype(BF16)


def slots_kernel(codes_ref, msg_ref, slot_ref):
    codes = codes_ref[...]
    blk = lax.shift_right_logical(codes, 11)
    off1 = jnp.bitwise_and(codes, K_OWN - 1) + 1
    sub = lax.broadcasted_iota(I32, (OWN, 128), 0)
    ht = jnp.concatenate(
        [onehot(sub == jnp.broadcast_to(blk[j : j + 1, :], (OWN, 128))) for j in range(8)], 1
    )
    upper = onehot(
        lax.broadcasted_iota(I32, (CELLS, CELLS), 0) < lax.broadcasted_iota(I32, (CELLS, CELLS), 1)
    )
    before = jnp.dot(ht, upper, preferred_element_type=F32)
    rank_row = jnp.sum(before * ht.astype(F32), axis=0, keepdims=True)
    rank = jnp.concatenate([rank_row[:, j * 128 : (j + 1) * 128] for j in range(8)], 0)
    slot_ref[...] = blk * CAP + rank.astype(I32)
    hi = lax.shift_right_logical(off1, 6).astype(F32)
    lo = jnp.bitwise_and(off1, 63).astype(F32)
    lane16 = jnp.bitwise_and(lax.broadcasted_iota(I32, (128, 128), 1), CAP - 1).astype(F32)
    v_hi, v_lo = [], []
    for j in range(8):

        def column(x):
            return jnp.transpose(jnp.broadcast_to(x[j : j + 1, :], (128, 128)))

        match = column(rank) == lane16
        v_hi.append(jnp.where(match, column(hi), 0.0).astype(BF16))
        v_lo.append(jnp.where(match, column(lo), 0.0).astype(BF16))
    m_hi = jnp.dot(ht, jnp.concatenate(v_hi, 0), preferred_element_type=F32)
    m_lo = jnp.dot(ht, jnp.concatenate(v_lo, 0), preferred_element_type=F32)
    msg_ref[...] = (m_hi * 64.0 + m_lo).astype(I32)


def make_slots(codes):
    vm = pl.BlockSpec(memory_space=pltpu.VMEM)
    return pl.pallas_call(
        slots_kernel,
        out_shape=(
            jax.ShapeDtypeStruct((OWN, 128), I32),
            jax.ShapeDtypeStruct((8, 128), I32),
        ),
        in_specs=[vm],
        out_specs=(vm, vm),
        compiler_params=pltpu.CompilerParams(vmem_limit_bytes=VMEM_LIMIT),
        name="slots",
    )(codes)


def norm_act(values):
    scaled = values * lax.rsqrt(jnp.mean(values * values, -1, keepdims=True) + 1e-06)
    return (scaled / (1.0 + jnp.exp(-scaled))).astype(BF16)


def conv_kernel(
    lat_ref,
    w1_ref,
    w2_ref,
    msg_ref,
    book_ref,
    enc_ref,
    rows_ref,
    wv,
    ext,
    cat,
    acc,
    first,
    rcodes,
    cbuf,
    sbuf,
    rbuf,
    w_sem,
    xs_sem,
    xr_sem,
    ts_sem,
    tr_sem,
    cs_sem,
    cr_sem,
    cb_sem,
    rs_sem,
    rr_sem,
    out_sem,
):
    t = lax.axis_index("tm")
    h = lax.axis_index("height")
    t_next, t_prev = lax.rem(t + 1, NT), lax.rem(t + NT - 1, NT)
    h_up, h_down = lax.rem(h + NH - 1, NH), lax.rem(h + 1, NH)

    barrier = pltpu.get_barrier_semaphore()
    pl.semaphore_signal(barrier, inc=1, device_id=(t_next, h), device_id_type=MESH)
    pl.semaphore_signal(barrier, inc=1, device_id=(t_prev, h), device_id_type=MESH)
    for i in range(1, NH):
        pl.semaphore_signal(
            barrier, inc=1, device_id=(t, lax.rem(h + i, NH)), device_id_type=MESH
        )

    for c, w_ref in enumerate((w1_ref, w2_ref)):
        for p in (2, 1, 0):
            for q in range(3):
                for r in range(3):
                    pltpu.make_async_copy(
                        w_ref.at[p, q, r],
                        wv.at[c, p, pl.ds(q * C, C), pl.ds(r * C, C)],
                        w_sem.at[c, p],
                    ).start()

    def weights_here(c, p):
        pltpu.make_async_copy(wv.at[c, p], wv.at[c, p], w_sem.at[c, p]).wait()

    def book_copy(g):
        return pltpu.make_async_copy(
            book_ref.at[pl.ds(g * K_OWN, K_OWN)], cbuf.at[g % 4], cb_sem.at[g % 4]
        )

    for g in range(4):
        book_copy(g).start()

    def x_copy(c, e, d):
        src, dst, to = ((1, 5, h_up), (4, 0, h_down))[d]
        return pltpu.make_async_remote_copy(
            src_ref=ext.at[c, e, src],
            dst_ref=ext.at[c, e, dst],
            send_sem=xs_sem.at[c, e, d],
            recv_sem=xr_sem.at[c, e, d],
            device_id=(t, to),
            device_id_type=MESH,
        )

    def t_copy(c, e):
        return pltpu.make_async_remote_copy(
            src_ref=ext.at[c, e + 2, pl.ds(1, 4)],
            dst_ref=ext.at[c, e, pl.ds(1, 4)],
            send_sem=ts_sem.at[c, e],
            recv_sem=tr_sem.at[c, e],
            device_id=(t_next, h),
            device_id_type=MESH,
        )

    def code_copy(i):
        to = lax.rem(h + i, NH)
        return pltpu.make_async_remote_copy(
            src_ref=msg_ref.at[pl.ds(pl.multiple_of(to * NT, NT), NT)],
            dst_ref=rcodes.at[h],
            send_sem=cs_sem.at[i],
            recv_sem=cr_sem.at[i],
            device_id=(t, to),
            device_id_type=MESH,
        )

    def row_copy(i, s):
        to = lax.rem(h + i, NH)
        return pltpu.make_async_remote_copy(
            src_ref=sbuf.at[to, pl.ds(s * 64, 64)],
            dst_ref=rbuf.at[h, pl.ds(s * 64, 64)],
            send_sem=rs_sem.at[i, s],
            recv_sem=rr_sem.at[i, s],
            device_id=(t, to),
            device_id_type=MESH,
        )

    def spread(c, e):
        for q in range(3):
            for i in range(4):
                x = ext[c, e, i + q]
                ok = None
                if e < 2:
                    ok = t > 0
                if q == 0 and i == 0:
                    ok = (h > 0) if ok is None else jnp.logical_and(ok, h > 0)
                if q == 2 and i == 3:
                    ok = (h < NH - 1) if ok is None else jnp.logical_and(ok, h < NH - 1)
                if ok is not None:
                    x = jnp.where(ok, x, jnp.zeros_like(x))
                cat[e, pl.ds(i * 128, 128), pl.ds(q * C, C)] = x

    def product(c, e, p):
        return jnp.dot(cat[e], wv[c, p], preferred_element_type=F32)

    col = lax.broadcasted_iota(I32, (128, C), 0)

    def finish(f, i, base):
        rows = pl.ds(i * 128, 128)
        left = pltpu.roll(acc[f, rows, pl.ds(0, C)], 1, 0)
        left = jnp.where(col == 0, 0.0, left)
        right = pltpu.roll(acc[f, rows, pl.ds(2 * C, C)], 127, 0)
        right = jnp.where(col == 127, 0.0, right)
        return (base.astype(F32) + ((left + right) + acc[f, rows, pl.ds(C, C)])).astype(BF16)

    for f in (1, 0):
        for i in range(4):
            ext[0, 2 + f, 1 + i] = norm_act(lat_ref[f, i].astype(F32))

    pl.semaphore_wait(barrier, NH + 1)
    for i in range(1, NH):
        code_copy(i).start()
    for e in (3, 2):
        for d in range(2):
            x_copy(0, e, d).start()
    t_copy(0, 1).start()
    t_copy(0, 0).start()
    rcodes[h] = msg_ref[pl.ds(pl.multiple_of(h * NT, NT), NT)]

    def fetch_rows():
        for i in range(1, NH):
            code_copy(i).wait_recv()
        lane_src = lax.shift_right_logical(lax.broadcasted_iota(I32, (NT, 128), 1), 4)
        rowmat = jnp.zeros((NT, 128), I32)
        for s in range(NH):
            rowmat = rowmat + jnp.where(lane_src == s, rcodes[s], 0)
        rowmat = rowmat.astype(F32) - 1.0
        lanes = lax.broadcasted_iota(I32, (128, 128), 1).astype(F32)
        for g in range(NT):
            book_copy(g).wait()
            column = jnp.transpose(jnp.broadcast_to(rowmat[g : g + 1, :], (128, 128)))
            pick = jnp.concatenate(
                [onehot(column - 128.0 * j == lanes) for j in range(K_OWN // 128)], 1
            )
            found = jnp.dot(pick, cbuf[g % 4], preferred_element_type=F32).astype(BF16)
            for s in range(NH):
                sbuf[s, pl.ds(g * CAP, CAP)] = found[s * CAP : (s + 1) * CAP]
            if g + 4 < NT:
                book_copy(g + 4).start()
            if g % 4 == 3:
                for i in range(1, NH):
                    row_copy(i, g // 4).start()
        rbuf[h] = sbuf[h]

    def conv(c, between):
        for e in (3, 2):
            for d in range(2):
                x_copy(c, e, d).wait_recv()
            spread(c, e)
        weights_here(c, 2)
        weights_here(c, 1)
        acc[1] = product(c, 3, 2)
        acc[1] += product(c, 2, 1)
        acc[0] = product(c, 2, 2)
        if between is not None:
            between()
        t_copy(c, 1).wait_recv()
        for d in range(2):
            x_copy(c, 1, d).start()
        for d in range(2):
            x_copy(c, 1, d).wait_recv()
        spread(c, 1)
        weights_here(c, 0)
        acc[1] += product(c, 1, 0)

    def tail(c):
        acc[0] += product(c, 1, 1)
        t_copy(c, 0).wait_recv()
        for d in range(2):
            x_copy(c, 0, d).start()
        for d in range(2):
            x_copy(c, 0, d).wait_recv()
        spread(c, 0)
        acc[0] += product(c, 0, 0)

    def next_frame(f):
        for i in range(4):
            x = finish(f, i, lat_ref[f, i])
            first[f, i] = x
            ext[1, 2 + f, 1 + i] = norm_act(x.astype(F32))
        for d in range(2):
            x_copy(1, 2 + f, d).start()
        t_copy(1, f).start()

    conv(0, fetch_rows)
    next_frame(1)
    tail(0)
    next_frame(0)
    conv(1, None)
    for i in range(4):
        enc_ref[1, i] = finish(1, i, first[1, i])
    tail(1)
    for i in range(4):
        enc_ref[0, i] = finish(0, i, first[0, i])

    for i in range(1, NH):
        for s in range(4):
            row_copy(i, s).wait_recv()
    out = pltpu.make_async_copy(rbuf, rows_ref, out_sem)
    out.start()
    for i in range(1, NH):
        code_copy(i).wait_send()
        for s in range(4):
            row_copy(i, s).wait_send()
    for c in range(2):
        for e in range(4):
            for d in range(2):
                x_copy(c, e, d).wait_send()
        for e in range(2):
            t_copy(c, e).wait_send()
    out.wait()


def conv_and_rows(latents, w1, w2, msg, book):
    vm = pl.BlockSpec(memory_space=pltpu.VMEM)
    hbm = pl.BlockSpec(memory_space=pl.ANY)
    dma = pltpu.SemaphoreType.DMA
    return pl.pallas_call(
        conv_kernel,
        out_shape=(
            jax.ShapeDtypeStruct((2, 4, 128, C), BF16),
            jax.ShapeDtypeStruct((NH, 256, C), BF16),
        ),
        in_specs=[vm, hbm, hbm, vm, hbm],
        out_specs=(vm, hbm),
        scratch_shapes=[
            pltpu.VMEM((2, 3, 3 * C, 3 * C), BF16),
            pltpu.VMEM((2, 4, 6, 128, C), BF16),
            pltpu.VMEM((4, 512, 3 * C), BF16),
            pltpu.VMEM((2, 512, 3 * C), F32),
            pltpu.VMEM((2, 4, 128, C), BF16),
            pltpu.VMEM((NH, NT, 128), I32),
            pltpu.VMEM((4, K_OWN, C), BF16),
            pltpu.VMEM((NH, 256, C), BF16),
            pltpu.VMEM((NH, 256, C), BF16),
            dma((2, 3)),
            dma((2, 4, 2)),
            dma((2, 4, 2)),
            dma((2, 2)),
            dma((2, 2)),
            dma((NH,)),
            dma((NH,)),
            dma((4,)),
            dma((NH, 4)),
            dma((NH, 4)),
            dma,
        ],
        compiler_params=pltpu.CompilerParams(
            collective_id=0, has_side_effects=True, vmem_limit_bytes=VMEM_LIMIT
        ),
        name="conv_and_rows",
    )(latents, w1, w2, msg, book)


def rotate_back(latent, quant, upward):
    lat_norm = jnp.sqrt(jnp.sum(latent * latent, -1, keepdims=True) + 1e-06)
    quant_norm = jnp.sqrt(jnp.sum(quant * quant, -1, keepdims=True) + 1e-06)
    lat_unit = latent / lat_norm
    quant_unit = quant / quant_norm
    cosine = jnp.sum(lat_unit * quant_unit, -1, keepdims=True)
    summed = lat_unit + quant_unit
    turned = upward - summed * (jnp.sum(summed * upward, -1, keepdims=True) / (1.0 + cosine))
    turned = turned + 2.0 * lat_unit * jnp.sum(quant_unit * upward, -1, keepdims=True)
    return quant_norm / lat_norm * turned + 0.5 * (latent - quant)


def grad_kernel(
    enc_ref,
    rows_ref,
    up_ref,
    msg_ref,
    slot_ref,
    grad_ref,
    sums_ref,
    tsend,
    trecv,
    crecv,
    slotcol,
    s_sem,
    r_sem,
    cs_sem,
    cr_sem,
    l_sem,
):
    t = lax.axis_index("tm")
    h = lax.axis_index("height")
    me = t * NH + h
    barrier = pltpu.get_barrier_semaphore()

    def partner(i):
        pt = lax.rem(t + lax.div(i, NH), NT)
        ph = lax.rem(h + lax.rem(i, NH), NH)
        return pt, ph

    @pl.loop(1, OWN)
    def _(i):
        pl.semaphore_signal(barrier, inc=1, device_id=partner(i), device_id_type=MESH)

    lane = lax.broadcasted_iota(I32, (256, 128), 0)
    slots = slot_ref[...]
    enc = enc_ref[...]

    for b in range(SLOTS // 256):
        pick = jnp.concatenate(
            [
                onehot(lane == jnp.broadcast_to(slots[j : j + 1, :], (256, 128)) - b * 256)
                for j in range(8)
            ],
            1,
        )
        placed = jnp.dot(pick, enc, preferred_element_type=F32)
        rows = pl.ds(b * 256, 256)
        tsend[rows] = (rows_ref[rows].astype(F32) - placed).astype(BF16)

    pl.semaphore_wait(barrier, OWN - 1)

    def code_copy(i):
        pt, ph = partner(i)
        return pltpu.make_async_remote_copy(
            src_ref=msg_ref.at[ph * NT + pt],
            dst_ref=crecv.at[me],
            send_sem=cs_sem,
            recv_sem=cr_sem,
            device_id=(pt, ph),
            device_id_type=MESH,
        )

    def term_copy(i):
        pt, ph = partner(i)
        return pltpu.make_async_remote_copy(
            src_ref=tsend.at[pl.ds(pl.multiple_of((ph * NT + pt) * CAP, CAP), CAP)],
            dst_ref=trecv.at[pl.ds(pl.multiple_of(me * CAP, CAP), CAP)],
            send_sem=s_sem,
            recv_sem=r_sem,
            device_id=(pt, ph),
            device_id_type=MESH,
        )

    @pl.loop(1, OWN)
    def _(i):
        code_copy(i).start()
        term_copy(i).start()

    own_codes = pltpu.make_async_copy(msg_ref.at[h * NT + t], crecv.at[me], cr_sem)
    own_codes.start()
    own_terms = pltpu.make_async_copy(
        tsend.at[pl.ds(pl.multiple_of((h * NT + t) * CAP, CAP), CAP)],
        trecv.at[pl.ds(pl.multiple_of(me * CAP, CAP), CAP)],
        r_sem,
    )
    own_terms.start()

    lanes = lax.broadcasted_iota(I32, (128, 128), 1).astype(F32)
    slots_f = slots.astype(F32)
    for j in range(8):
        column = jnp.transpose(jnp.broadcast_to(slots_f[j : j + 1, :], (128, 128)))
        pick = jnp.concatenate(
            [onehot(column - 128.0 * k == lanes) for k in range(SLOTS // 128)], 1
        )
        quant = jnp.dot(pick, rows_ref[...], preferred_element_type=F32)
        cells = pl.ds(j * 128, 128)
        grad_ref[cells] = rotate_back(
            enc_ref[cells].astype(F32), quant, up_ref[cells].astype(F32)
        ).astype(BF16)

    pltpu.make_async_copy(crecv, crecv, cr_sem).wait()
    group = lax.broadcasted_iota(I32, (8, 128), 0)
    mine = lax.shift_right_logical(lax.broadcasted_iota(I32, (8, 128), 1), 4) == group
    row_of = []
    for j in range(SLOTS // 128):
        tile = crecv[pl.ds(j * 8, 8)]
        row_of.append(jnp.sum(jnp.where(mine, tile, 0), axis=0, keepdims=True) - 1)

    pltpu.make_async_copy(trecv, trecv, r_sem).wait()
    for b in range(K_OWN // 256):
        pick = jnp.concatenate(
            [onehot(lane == jnp.broadcast_to(r - b * 256, (256, 128))) for r in row_of], 1
        )
        sums = jnp.dot(pick, trecv[...], preferred_element_type=F32)
        sums_ref[pl.ds(b * 256, 256)] = (2.0 * sums).astype(BF16)

    @pl.loop(1, OWN)
    def _(i):
        code_copy(i).wait_send()
        term_copy(i).wait_send()


def gradients(enc, rows, upstream, msg, slot):
    vm = pl.BlockSpec(memory_space=pltpu.VMEM)
    dma = pltpu.SemaphoreType.DMA
    return pl.pallas_call(
        grad_kernel,
        out_shape=(
            jax.ShapeDtypeStruct((CELLS, C), BF16),
            jax.ShapeDtypeStruct((K_OWN, C), BF16),
        ),
        in_specs=[vm] * 5,
        out_specs=(vm, vm),
        scratch_shapes=[
            pltpu.VMEM((SLOTS, C), BF16),
            pltpu.VMEM((SLOTS, C), BF16),
            pltpu.VMEM((OWN, 128), I32),
            pltpu.VMEM((8, 128), F32),
            dma,
            dma,
            dma,
            dma,
            dma,
        ],
        compiler_params=pltpu.CompilerParams(
            collective_id=1, has_side_effects=True, vmem_limit_bytes=VMEM_LIMIT
        ),
        name="gradients",
    )(enc, rows, upstream, msg, slot)


def on_device(latents, conv_first, conv_second, codebook, codes, upstream):
    msg, slot = make_slots(codes.reshape(8, 128))
    enc, rows = conv_and_rows(latents, conv_first, conv_second, msg, codebook)
    grad, sums = gradients(
        enc.reshape(CELLS, C), rows.reshape(SLOTS, C), upstream.reshape(CELLS, C), msg, slot
    )
    return grad.reshape(upstream.shape), sums


def solution(mesh):
    return jax.shard_map(
        on_device,
        mesh=mesh,
        in_specs=(
            P("tm", "height", None, None),
            P(),
            P(),
            P("height", None),
            P("tm", "height", None),
            P("tm", "height", None, None),
        ),
        out_specs=(P("tm", "height", None, None), P(("height", "tm"), None)),
        check_vma=False,
    )
```

time: 184 us -> 91 us (0.49)
  Pallas kernels: 0 us -> 84.7 us
  other arithmetic: 47.2 us -> 0 us
  starting transfers between devices: 46.8 us -> 0 us
  local copies, waits for them, and re-layouts: 48.5 us -> 4.13 us
  waiting for transfers between devices: 30.3 us -> 0 us
  matrix products: 8.41 us -> 0 us
    pallas_call x0 -> x3, Pallas kernels: none -> 84.7 us  [the longest x1 54.1 us: conv_and_rows(): pl.pallas_call(conv_kernel, out_shape=(jax.ShapeDtypeStruct((2, 4, 128, C...]
    all_to_all x3 -> x0, starting transfers between devices: 27.3 us -> none  [the longest x1 11.4 us: on_device(): lax.all_to_all(term_slots.reshape(owners, capacity, channels), ('tm', 'he...]
    gather x2 -> x0, local copies, waits for them, and re-layouts: 22.4 us -> none  [the longest x1 16.4 us: on_device(): found_rows = jnp.take(codebook, local_rows, axis=0)]
    all_to_all x3 -> x0, waiting for transfers between devices: 21 us -> none  [the longest x1 13 us: on_device(): lax.all_to_all(term_slots.reshape(owners, capacity, channels), ('tm', 'he...]
    ppermute x6 -> x0, starting transfers between devices: 19.5 us -> none  [the longest x2 8.11 us: passed_along(): return lax.ppermute(x, axis, pairs)]
    scatter-add x1 -> x0, other arithmetic: 12.4 us -> none  [on_device(): sums = jnp.zeros((range_rows, channels), jnp.float32).at[target_rows.resh...]
    scatter x2 -> x0, local copies, waits for them, and re-layouts: 10.9 us -> none  [the longest x1 6.41 us: on_device(): jnp.zeros((owners * capacity, channels), jnp.bfloat16).at[slot_index]]
    ppermute x6 -> x0, waiting for transfers between devices: 9.31 us -> none  [the longest x2 9.3 us: passed_along(): return lax.ppermute(x, axis, pairs)]
  transfers between devices with their start and end apart: 9 -> 0, of which waited for: 3 -> 0; matrix products, arithmetic and copies ran while one was open for 35% -> 0% of each run, Pallas kernels for 0% -> 0%
where the time goes in v1:
time: 91 us; the launch traced here: 89.5 us
  Pallas kernels  84.7 us (93%)
  local copies, waits for them, and re-layouts  4.13 us (5%)
    pallas_call x1, Pallas kernels, conv_and_rows(): pl.pallas_call(conv_kernel, out_shape=(jax.ShapeDtypeStruct((2, 4, 128, C...  54.1 us
    pallas_call x1, Pallas kernels, gradients(): pl.pallas_call(grad_kernel, out_shape=(jax.ShapeDtypeStruct((CELLS, C), B...  28.3 us
    unnamed x2, local copies, waits for them, and re-layouts  4.13 us
    pallas_call x1, Pallas kernels, make_slots(): pl.pallas_call(slots_kernel, out_shape=(jax.ShapeDtypeStruct((OWN, 128),...  2.25 us

profile of v1, /device:TPU:1, one launch (start us, length us, event | category | flops | bytes accessed | tf_op | source)
XLA Modules:
  0.0 89.5 jit_solution(6554247749118185679)
XLA Ops:
  0.6 2.3 %slots.1 = (s32[128,128]{1,0:T(8,128)}, s32[8,128]{1,0:T(8,128)}) custom-call(s32[8,128]{1,0:T(8,128)} %bitcast.9), custom_call_target="tpu_custom_call" | custom-call | tf_op jit(solution)/shard_map/slots/pallas_call | solution.py:62
  2.9 54.1 %conv_and_rows.1 = (bf16[2,4,128,256]{3,2,1,0:T(8,128)(2,1)}, bf16[8,256,256]{2,1,0:T(8,128)(2,1)}) custom-call(bf16[2,4,128,256]{3,2,1,0:T(8,128)(2,1)} %lat_ref.1, bf16[3,3,3,256,256]{4,3,2,1,0:T(8,128)(2,1)} %w1_ref.1, bf16[3,3,3,256,256]{4,3,2,1,0:T(8,128)(2,1)} %w2_ref.1, s32[128,128]{1,0:T(8,128)} %get-tuple-element.8.msg_ref, bf16[32768,256]{1,0:T(8,128)(2,1)} %book_ref.1), custom_call_target="tpu_custom_call" | custom-call | tf_op jit(solution)/shard_map/conv_and_rows/pallas_call | solution.py:326
  57.0 28.3 %gradients.1 = (bf16[1024,256]{1,0:T(8,128)(2,1)}, bf16[2048,256]{1,0:T(8,128)(2,1)}) custom-call(bf16[1024,256]{1,0:T(8,128)(2,1)} %bitcast.8, bf16[2048,256]{1,0:T(8,128)(2,1)} %bitcast.5, bf16[1024,256]{1,0:T(8,128)(2,1)} %bitcast.7, s32[128,128]{1,0:T(8,128)} %get-tuple-element.8.msg_ref, s32[8,128]{1,0:T(8,128)} %get-tuple-element.11.slot_ref), custom_call_target="tpu_custom_call" | custom-call | tf_op jit(solution)/shard_map/gradients/pallas_call | solution.py:499
  85.4 1.9 %copy.10 = bf16[2,4,128,256]{3,2,1,0:T(8,128)(2,1)} copy(bf16[2,4,128,256]{3,2,1,0:T(8,128)(2,1)} %bitcast.6) | data formatting | bytes 1048576
  87.2 2.3 %copy.11 = bf16[2048,256]{1,0:T(8,128)(2,1)} copy(bf16[2048,256]{1,0:T(8,128)(2,1)} %get-tuple-element.17) | data formatting | bytes 2097152

commit v2 on v0

v2 whole, which is shorter than its diff:
```python
import functools

import jax
import jax.numpy as jnp
from jax import lax
from jax.experimental import pallas as pl
from jax.experimental.pallas import tpu as pltpu
from jax.sharding import PartitionSpec as P

F32 = jnp.float32
BF16 = jnp.bfloat16
I32 = jnp.int32
MESH = pl.DeviceIdType.MESH
C = 256
NT, NH = 16, 8
OWN = NT * NH
CAP = 16
SLOTS = OWN * CAP
K_OWN = 2048
CELLS = 1024
VMEM_LIMIT = 60 * 1024 * 1024


def onehot(cond):
    return jnp.where(cond, 1.0, 0.0).astype(BF16)


def norm_act(values):
    scaled = values * lax.rsqrt(jnp.mean(values * values, -1, keepdims=True) + 1e-06)
    return (scaled / (1.0 + jnp.exp(-scaled))).astype(BF16)


def rotate_back(latent, quant, upward):
    lat_norm = jnp.sqrt(jnp.sum(latent * latent, -1, keepdims=True) + 1e-06)
    quant_norm = jnp.sqrt(jnp.sum(quant * quant, -1, keepdims=True) + 1e-06)
    lat_unit = latent / lat_norm
    quant_unit = quant / quant_norm
    cosine = jnp.sum(lat_unit * quant_unit, -1, keepdims=True)
    summed = lat_unit + quant_unit
    turned = upward - summed * (jnp.sum(summed * upward, -1, keepdims=True) / (1.0 + cosine))
    turned = turned + 2.0 * lat_unit * jnp.sum(quant_unit * upward, -1, keepdims=True)
    return quant_norm / lat_norm * turned + 0.5 * (latent - quant)


def column(row):
    return jnp.transpose(jnp.broadcast_to(row, (128, 128)))


def window_kernel(
    lat_hbm,
    w1_ref,
    w2_ref,
    book_ref,
    codes_ref,
    up_hbm,
    grad_hbm,
    sums_hbm,
    lat,
    up,
    wv,
    ext,
    cat,
    acc,
    first,
    enc,
    msg,
    slot,
    rcodes,
    cbuf,
    sbuf,
    rbuf,
    place,
    placed,
    tsend,
    trecv,
    crecv,
    spread_in,
    sums,
    sums_out,
    grad_out,
    in_sem,
    w_sem,
    xs_sem,
    xr_sem,
    ts_sem,
    tr_sem,
    cs_sem,
    cr_sem,
    cb_sem,
    rs_sem,
    rr_sem,
    ks_sem,
    kr_sem,
    gs_sem,
    gr_sem,
    out_sem,
    know,
):
    t = lax.axis_index("tm")
    h = lax.axis_index("height")
    h_up, h_down = lax.rem(h + NH - 1, NH), lax.rem(h + 1, NH)

    def at_t(by):
        return lax.rem(t + NT + by, NT)

    def at_h(by):
        return lax.rem(h + by, NH)

    barrier = pltpu.get_barrier_semaphore()
    for by in (1, -1):
        pl.semaphore_signal(barrier, inc=1, device_id=(at_t(by), h), device_id_type=MESH)
    for i in range(1, NH):
        pl.semaphore_signal(barrier, inc=1, device_id=(t, at_h(i)), device_id_type=MESH)

    lat_in = [pltpu.make_async_copy(lat_hbm.at[f], lat.at[f], in_sem.at[f]) for f in range(2)]
    up_in = pltpu.make_async_copy(up_hbm, up, in_sem.at[2])
    lat_in[1].start()
    lat_in[0].start()

    def weights_start(c, p):
        w_ref = (w1_ref, w2_ref)[c]
        for q in range(3):
            for r in range(3):
                pltpu.make_async_copy(
                    w_ref.at[p, q, r],
                    wv.at[c, p, pl.ds(q * C, C), pl.ds(r * C, C)],
                    w_sem.at[c, p],
                ).start()

    def weights_here(c, p):
        pltpu.make_async_copy(wv.at[c, p], wv.at[c, p], w_sem.at[c, p]).wait()

    def book_copy(g):
        return pltpu.make_async_copy(
            book_ref.at[pl.ds(g * K_OWN, K_OWN)], cbuf.at[g % 4], cb_sem.at[g % 4]
        )

    def x_copy(c, e, d):
        src, dst, to = ((1, 5, h_up), (4, 0, h_down))[d]
        return pltpu.make_async_remote_copy(
            src_ref=ext.at[c, e, src],
            dst_ref=ext.at[c, e, dst],
            send_sem=xs_sem.at[c, e, d],
            recv_sem=xr_sem.at[c, e, d],
            device_id=(t, to),
            device_id_type=MESH,
        )

    def t_copy(c, e, part):
        rows = (pl.ds(1, 1), pl.ds(4, 1), pl.ds(2, 2))[part]
        return pltpu.make_async_remote_copy(
            src_ref=ext.at[c, e + 2, rows],
            dst_ref=ext.at[c, e, rows],
            send_sem=ts_sem.at[c, e, part],
            recv_sem=tr_sem.at[c, e, part],
            device_id=(at_t(1), h),
            device_id_type=MESH,
        )

    def code_copy(i):
        to = at_h(i)
        return pltpu.make_async_remote_copy(
            src_ref=msg.at[pl.ds(pl.multiple_of(to * NT, NT), NT)],
            dst_ref=rcodes.at[h],
            send_sem=cs_sem.at[i],
            recv_sem=cr_sem.at[i],
            device_id=(t, to),
            device_id_type=MESH,
        )

    def row_copy(i, s):
        to = at_h(i)
        return pltpu.make_async_remote_copy(
            src_ref=sbuf.at[to, pl.ds(s * 64, 64)],
            dst_ref=rbuf.at[h, pl.ds(s * 64, 64)],
            send_sem=rs_sem.at[i, s],
            recv_sem=rr_sem.at[i, s],
            device_id=(t, to),
            device_id_type=MESH,
        )

    def owner(i, dt):
        to_t, to_h = lax.rem(t + dt, NT), at_h(i)
        return to_t, to_h, to_h * NT + to_t

    def key_copy(i, dt):
        to_t, to_h, blk = owner(i, dt)
        return pltpu.make_async_remote_copy(
            src_ref=msg.at[blk],
            dst_ref=crecv.at[i * NT + t],
            send_sem=ks_sem,
            recv_sem=kr_sem,
            device_id=(to_t, to_h),
            device_id_type=MESH,
        )

    def term_copy(i, dt):
        to_t, to_h, blk = owner(i, dt)
        return pltpu.make_async_remote_copy(
            src_ref=tsend.at[pl.ds(pl.multiple_of(blk * CAP, CAP), CAP)],
            dst_ref=trecv.at[pl.ds(pl.multiple_of((i * NT + t) * CAP, CAP), CAP)],
            send_sem=gs_sem,
            recv_sem=gr_sem.at[i // 4],
            device_id=(to_t, to_h),
            device_id_type=MESH,
        )

    def widen(c, e):
        for q in range(3):
            for i in range(4):
                x = ext[c, e, i + q]
                ok = None
                if e < 2:
                    ok = t > 0
                if q == 0 and i == 0:
                    ok = (h > 0) if ok is None else jnp.logical_and(ok, h > 0)
                if q == 2 and i == 3:
                    ok = (h < NH - 1) if ok is None else jnp.logical_and(ok, h < NH - 1)
                if ok is not None:
                    x = jnp.where(ok, x, jnp.zeros_like(x))
                cat[e, pl.ds(i * 128, 128), pl.ds(q * C, C)] = x

    def product(c, e, p):
        return jnp.dot(cat[e], wv[c, p], preferred_element_type=F32)

    col = lax.broadcasted_iota(I32, (128, C), 0)

    def finish(f, i, base):
        rows = pl.ds(i * 128, 128)
        left = pltpu.roll(acc[f, rows, pl.ds(0, C)], 1, 0)
        left = jnp.where(col == 0, 0.0, left)
        right = pltpu.roll(acc[f, rows, pl.ds(2 * C, C)], 127, 0)
        right = jnp.where(col == 127, 0.0, right)
        return (base.astype(F32) + ((left + right) + acc[f, rows, pl.ds(C, C)])).astype(BF16)

    def send_frame(c, f):
        for d in range(2):
            x_copy(c, 2 + f, d).start()
        for part in range(3):
            t_copy(c, f, part).start()

    lane_i = lax.broadcasted_iota(I32, (128, 128), 1)
    lanes = lane_i.astype(F32)

    def make_slots():
        codes = codes_ref[...]
        blk = lax.shift_right_logical(codes, 11)
        off1 = jnp.bitwise_and(codes, K_OWN - 1) + 1
        sub = lax.broadcasted_iota(I32, (OWN, 128), 0)
        ht = jnp.concatenate(
            [onehot(sub == jnp.broadcast_to(blk[j : j + 1, :], (OWN, 128))) for j in range(8)], 1
        )
        upper = onehot(
            lax.broadcasted_iota(I32, (CELLS, CELLS), 0)
            < lax.broadcasted_iota(I32, (CELLS, CELLS), 1)
        )
        before = jnp.dot(ht, upper, preferred_element_type=F32)
        rank_row = jnp.sum(before * ht.astype(F32), axis=0, keepdims=True)
        rank = jnp.concatenate([rank_row[:, j * 128 : (j + 1) * 128] for j in range(8)], 0)
        slot[...] = blk * CAP + rank.astype(I32)
        hi = lax.shift_right_logical(off1, 6).astype(F32)
        lo = jnp.bitwise_and(off1, 63).astype(F32)
        lane16 = jnp.bitwise_and(lane_i, CAP - 1).astype(F32)
        v_hi, v_lo = [], []
        for j in range(8):
            match = column(rank[j : j + 1, :]) == lane16
            v_hi.append(jnp.where(match, column(hi[j : j + 1, :]), 0.0).astype(BF16))
            v_lo.append(jnp.where(match, column(lo[j : j + 1, :]), 0.0).astype(BF16))
        m_hi = jnp.dot(ht, jnp.concatenate(v_hi, 0), preferred_element_type=F32)
        m_lo = jnp.dot(ht, jnp.concatenate(v_lo, 0), preferred_element_type=F32)
        msg[...] = (m_hi * 64.0 + m_lo).astype(I32)

    def asked_rows():
        for i in range(1, NH):
            code_copy(i).wait_recv()
        lane_src = lax.shift_right_logical(lax.broadcasted_iota(I32, (NT, 128), 1), 4)
        rowmat = jnp.zeros((NT, 128), I32)
        for s in range(NH):
            rowmat = rowmat + jnp.where(lane_src == s, rcodes[s], 0)
        return rowmat.astype(F32) - 1.0

    def gather(rowmat, k):
        for g in range(4 * k, 4 * k + 4):
            book_copy(g).wait()
            want = column(rowmat[g : g + 1, :])
            pick = jnp.concatenate(
                [onehot(want - 128.0 * j == lanes) for j in range(K_OWN // 128)], 1
            )
            found = jnp.dot(pick, cbuf[g % 4], preferred_element_type=F32).astype(BF16)
            for s in range(NH):
                sbuf[s, pl.ds(g * CAP, CAP)] = found[s * CAP : (s + 1) * CAP]
            if g + 4 < NT:
                book_copy(g + 4).start()

    def send_rows(k):
        for i in range(1, NH):
            row_copy(i, k).start()

    def tell(r, by):
        for sign in (1, -1):
            pl.semaphore_signal(
                know.at[r], inc=1, device_id=(at_t(sign * by), h), device_id_type=MESH
            )

    lane = lax.broadcasted_iota(I32, (256, 128), 0)

    def make_place():
        @pl.loop(0, SLOTS // 256)
        def _(b):
            rows = pl.ds(pl.multiple_of(b * 256, 256), 256)
            for j in range(8):
                row = slot[pl.ds(j, 1), :] - b * 256
                place[j // 4, rows, pl.ds((j % 4) * 128, 128)] = onehot(
                    lane == jnp.broadcast_to(row, (256, 128))
                )

    def make_spread():
        pltpu.make_async_copy(crecv, crecv, kr_sem).wait()
        group = lax.broadcasted_iota(I32, (8, 128), 0)
        mine = lax.shift_right_logical(lax.broadcasted_iota(I32, (8, 128), 1), 4) == group
        row_of = []
        for j in range(SLOTS // 128):
            tile = crecv[pl.ds(j * 8, 8)]
            row_of.append(jnp.sum(jnp.where(mine, tile, 0), axis=0, keepdims=True) - 1)

        @pl.loop(0, K_OWN // 256)
        def _(b):
            rows = pl.ds(pl.multiple_of(b * 256, 256), 256)
            for j in range(SLOTS // 128):
                spread_in[rows, pl.ds(j * 128, 128)] = onehot(
                    lane == jnp.broadcast_to(row_of[j] - b * 256, (256, 128))
                )

    for f in (1, 0):
        lat_in[f].wait()
        for i in range(4):
            ext[0, 2 + f, 1 + i] = norm_act(lat[f, i].astype(F32))
        if f == 1:
            pl.semaphore_wait(barrier, NH + 1)
        send_frame(0, f)
    tell(0, 1)
    for c in range(2):
        for p in (2, 1, 0):
            weights_start(c, p)
        if c == 0:
            for g in range(4):
                book_copy(g).start()
    up_in.start()

    make_slots()
    for i in range(1, NH):
        code_copy(i).start()
    rcodes[h] = msg[pl.ds(pl.multiple_of(h * NT, NT), NT)]

    def local_part(c):
        for e in (3, 2):
            for d in range(2):
                x_copy(c, e, d).wait_recv()
            widen(c, e)
        if c == 1:
            send_rows(2)
        weights_here(c, 2)
        weights_here(c, 1)
        acc[1] = product(c, 3, 2)
        acc[1] += product(c, 2, 1)
        acc[0] = product(c, 2, 2)

    def earlier_frame(c, e, between, rows_piece):
        for d in range(2):
            t_copy(c, e, d).wait_recv()
            x_copy(c, e, d).start()
        if between is not None:
            between()
        t_copy(c, e, 2).wait_recv()
        for d in range(2):
            x_copy(c, e, d).wait_recv()
        if rows_piece is not None:
            send_rows(rows_piece)
        widen(c, e)
        if e == 1:
            weights_here(c, 0)
            acc[1] += product(c, 1, 0)
        else:
            acc[0] += product(c, 0, 0)

    def next_frame(f):
        for i in range(4):
            x = finish(f, i, lat[f, i])
            first[f, i] = x
            ext[1, 2 + f, 1 + i] = norm_act(x.astype(F32))
        send_frame(1, f)

    local_part(0)
    rowmat = asked_rows()
    gather(rowmat, 0)
    gather(rowmat, 1)
    pl.semaphore_wait(know.at[0], 2)
    tell(1, 2)
    earlier_frame(0, 1, lambda: gather(rowmat, 2), 0)
    next_frame(1)
    acc[0] += product(0, 1, 1)
    pl.semaphore_wait(know.at[1], 2)
    tell(2, 4)
    gather(rowmat, 3)
    rbuf[h] = sbuf[h]
    earlier_frame(0, 0, None, 1)
    next_frame(0)

    pl.semaphore_wait(know.at[2], 2)
    for i in range(1, NH):
        pl.semaphore_signal(know.at[3], inc=1, device_id=(t, at_h(i)), device_id_type=MESH)
    make_place()
    local_part(1)

    def send_keys():
        pl.semaphore_wait(know.at[3], NH - 1)
        for i in range(NH):

            @pl.loop(1 if i == 0 else 0, NT)
            def _(dt):
                key_copy(i, dt).start()

        pltpu.make_async_copy(msg.at[h * NT + t], crecv.at[t], kr_sem).start()

    send_keys()
    earlier_frame(1, 1, None, 3)
    for i in range(4):
        enc[1, pl.ds(i * 128, 128)] = finish(1, i, first[1, i])
    acc[0] += product(1, 1, 1)
    placed[...] = jnp.dot(place[1], enc[1], preferred_element_type=F32)
    make_spread()
    earlier_frame(1, 0, None, None)
    for i in range(4):
        enc[0, pl.ds(i * 128, 128)] = finish(0, i, first[0, i])

    for s in range(4):
        for i in range(1, NH):
            row_copy(i, s).wait_recv()

    for i in range(NH):
        to_h = at_h(i)
        rows = pl.ds(pl.multiple_of(to_h * 256, 256), 256)
        total = placed[rows] + jnp.dot(place[0, rows], enc[0], preferred_element_type=F32)
        tsend[rows] = (rbuf[to_h].astype(F32) - total).astype(BF16)

        @pl.loop(1 if i == 0 else 0, NT)
        def _(dt):
            term_copy(i, dt).start()

        if i == 0:
            pltpu.make_async_copy(
                tsend.at[pl.ds(pl.multiple_of((h * NT + t) * CAP, CAP), CAP)],
                trecv.at[pl.ds(pl.multiple_of(t * CAP, CAP), CAP)],
                gr_sem.at[0],
            ).start()

    up_in.wait()
    rows_all = rbuf[...].reshape(SLOTS, C)
    for j in range(8):
        want = column(slot[pl.ds(j, 1), :].astype(F32))
        pick = jnp.concatenate([onehot(want - 128.0 * k == lanes) for k in range(SLOTS // 128)], 1)
        quant = jnp.dot(pick, rows_all, preferred_element_type=F32)
        cells = pl.ds((j % 4) * 128, 128)
        grad_out[pl.ds(j * 128, 128)] = rotate_back(
            enc[j // 4, cells].astype(F32), quant, up[pl.ds(j * 128, 128)].astype(F32)
        ).astype(BF16)
    grad_done = pltpu.make_async_copy(grad_out, grad_hbm, out_sem.at[0])
    grad_done.start()

    half = SLOTS // 2
    low, high = pl.ds(0, half), pl.ds(half, half)
    pltpu.make_async_copy(trecv.at[low], trecv.at[low], gr_sem.at[0]).wait()
    sums[...] = jnp.dot(spread_in[:, low], trecv[low], preferred_element_type=F32)
    pltpu.make_async_copy(trecv.at[high], trecv.at[high], gr_sem.at[1]).wait()
    done = []
    for b in range(4):
        rows = pl.ds(b * 512, 512)
        total = sums[rows] + jnp.dot(
            spread_in[rows, high], trecv[high], preferred_element_type=F32
        )
        sums_out[rows] = (2.0 * total).astype(BF16)
        copy = pltpu.make_async_copy(sums_out.at[rows], sums_hbm.at[rows], out_sem.at[1 + b])
        copy.start()
        done.append(copy)

    for i in range(1, NH):
        code_copy(i).wait_send()
        for s in range(4):
            row_copy(i, s).wait_send()
    for c in range(2):
        for e in range(4):
            for d in range(2):
                x_copy(c, e, d).wait_send()
        for e in range(2):
            for part in range(3):
                t_copy(c, e, part).wait_send()
    sent = pl.ds(0, SLOTS - CAP)
    pltpu.make_async_copy(tsend.at[sent], tsend.at[sent], gs_sem).wait()
    sent = pl.ds(0, OWN - 1)
    pltpu.make_async_copy(crecv.at[sent], crecv.at[sent], ks_sem).wait()
    grad_done.wait()
    for copy in done:
        copy.wait()


def window(latents, w1, w2, book, codes, upstream):
    vm = pl.BlockSpec(memory_space=pltpu.VMEM)
    hbm = pl.BlockSpec(memory_space=pl.ANY)
    dma = pltpu.SemaphoreType.DMA
    return pl.pallas_call(
        window_kernel,
        out_shape=(
            jax.ShapeDtypeStruct((CELLS, C), BF16),
            jax.ShapeDtypeStruct((K_OWN, C), BF16),
        ),
        in_specs=[hbm, hbm, hbm, hbm, vm, hbm],
        out_specs=(hbm, hbm),
        scratch_shapes=[
            pltpu.VMEM((2, 4, 128, C), BF16),
            pltpu.VMEM((CELLS, C), BF16),
            pltpu.VMEM((2, 3, 3 * C, 3 * C), BF16),
            pltpu.VMEM((2, 4, 6, 128, C), BF16),
            pltpu.VMEM((4, 512, 3 * C), BF16),
            pltpu.VMEM((2, 512, 3 * C), F32),
            pltpu.VMEM((2, 4, 128, C), BF16),
            pltpu.VMEM((2, 512, C), BF16),
            pltpu.VMEM((OWN, 128), I32),
            pltpu.VMEM((8, 128), I32),
            pltpu.VMEM((NH, NT, 128), I32),
            pltpu.VMEM((4, K_OWN, C), BF16),
            pltpu.VMEM((NH, 256, C), BF16),
            pltpu.VMEM((NH, 256, C), BF16),
            pltpu.VMEM((2, SLOTS, 512), BF16),
            pltpu.VMEM((SLOTS, C), F32),
            pltpu.VMEM((SLOTS, C), BF16),
            pltpu.VMEM((SLOTS, C), BF16),
            pltpu.VMEM((OWN, 128), I32),
            pltpu.VMEM((K_OWN, SLOTS), BF16),
            pltpu.VMEM((K_OWN, C), F32),
            pltpu.VMEM((K_OWN, C), BF16),
            pltpu.VMEM((CELLS, C), BF16),
            dma((3,)),
            dma((2, 3)),
            dma((2, 4, 2)),
            dma((2, 4, 2)),
            dma((2, 2, 3)),
            dma((2, 2, 3)),
            dma((NH,)),
            dma((NH,)),
            dma((4,)),
            dma((NH, 4)),
            dma((NH, 4)),
            dma,
            dma,
            dma,
            dma((2,)),
            dma((5,)),
            pltpu.SemaphoreType.REGULAR((4,)),
        ],
        compiler_params=pltpu.CompilerParams(
            collective_id=0, has_side_effects=True, vmem_limit_bytes=VMEM_LIMIT
        ),
        name="window",
    )(latents, w1, w2, book, codes, upstream)


def hand_kernel(grad_in, sums_in, grad_ref, sums_ref, grad_buf, sums_buf, in_sem, out_sem):
    pieces = [(grad_in, grad_buf, grad_ref, 0), (grad_in, grad_buf, grad_ref, 1)] + [
        (sums_in, sums_buf, sums_ref, k) for k in range(4)
    ]
    ins, outs = [], []
    for n, (src, buf, dst, k) in enumerate(pieces):
        rows = pl.ds(k * 512, 512)
        ins.append(pltpu.make_async_copy(src.at[rows], buf.at[rows], in_sem.at[n]))
        outs.append(pltpu.make_async_copy(buf.at[rows], dst.at[rows], out_sem.at[n]))
        ins[-1].start()
    for n in range(len(pieces)):
        ins[n].wait()
        outs[n].start()
    for n in range(len(pieces)):
        outs[n].wait()


def hand_over(grad, sums):
    hbm = pl.BlockSpec(memory_space=pl.ANY)
    dma = pltpu.SemaphoreType.DMA
    return pl.pallas_call(
        hand_kernel,
        out_shape=(
            jax.ShapeDtypeStruct((CELLS, C), BF16),
            jax.ShapeDtypeStruct((K_OWN, C), BF16),
        ),
        in_specs=[hbm, hbm],
        out_specs=(hbm, hbm),
        scratch_shapes=[
            pltpu.VMEM((CELLS, C), BF16),
            pltpu.VMEM((K_OWN, C), BF16),
            dma((6,)),
            dma((6,)),
        ],
        name="hand_over",
    )(grad, sums)


def on_device(latents, conv_first, conv_second, codebook, codes, upstream):
    grad, sums = window(
        latents,
        conv_first,
        conv_second,
        codebook,
        codes.reshape(8, 128),
        upstream.reshape(CELLS, C),
    )
    grad, sums = hand_over(grad, sums)
    return grad.reshape(upstream.shape), sums


def solution(mesh):
    return jax.shard_map(
        on_device,
        mesh=mesh,
        in_specs=(
            P("tm", "height", None, None),
            P(),
            P(),
            P("height", None),
            P("tm", "height", None),
            P("tm", "height", None, None),
        ),
        out_specs=(P("tm", "height", None, None), P(("height", "tm"), None)),
        check_vma=False,
    )
```

time: 184 us -> 74.7 us (0.41)
  Pallas kernels: 0 us -> 73.7 us
  local copies, waits for them, and re-layouts: 48.5 us -> 0 us
  other arithmetic: 47.2 us -> 0 us
  starting transfers between devices: 46.8 us -> 0 us
  waiting for transfers between devices: 30.3 us -> 0 us
  matrix products: 8.41 us -> 0 us
    pallas_call x0 -> x2, Pallas kernels: none -> 73.7 us  [the longest x1 71.5 us: window(): pl.pallas_call(window_kernel, out_shape=(jax.ShapeDtypeStruct((CELLS, C),...]
    all_to_all x3 -> x0, starting transfers between devices: 27.3 us -> none  [the longest x1 11.4 us: on_device(): lax.all_to_all(term_slots.reshape(owners, capacity, channels), ('tm', 'he...]
    gather x2 -> x0, local copies, waits for them, and re-layouts: 22.4 us -> none  [the longest x1 16.4 us: on_device(): found_rows = jnp.take(codebook, local_rows, axis=0)]
    all_to_all x3 -> x0, waiting for transfers between devices: 21 us -> none  [the longest x1 13 us: on_device(): lax.all_to_all(term_slots.reshape(owners, capacity, channels), ('tm', 'he...]
    ppermute x6 -> x0, starting transfers between devices: 19.5 us -> none  [the longest x2 8.11 us: passed_along(): return lax.ppermute(x, axis, pairs)]
    scatter-add x1 -> x0, other arithmetic: 12.4 us -> none  [on_device(): sums = jnp.zeros((range_rows, channels), jnp.float32).at[target_rows.resh...]
    scatter x2 -> x0, local copies, waits for them, and re-layouts: 10.9 us -> none  [the longest x1 6.41 us: on_device(): jnp.zeros((owners * capacity, channels), jnp.bfloat16).at[slot_index]]
    ppermute x6 -> x0, waiting for transfers between devices: 9.31 us -> none  [the longest x2 9.3 us: passed_along(): return lax.ppermute(x, axis, pairs)]
  transfers between devices with their start and end apart: 9 -> 0, of which waited for: 3 -> 0; matrix products, arithmetic and copies ran while one was open for 35% -> 0% of each run, Pallas kernels for 0% -> 0%
where the time goes in v2:
time: 74.7 us; the launch traced here: 74.5 us
  Pallas kernels  73.7 us (99%)
  between operations  0.8 us (1%)
    pallas_call x1, Pallas kernels, window(): pl.pallas_call(window_kernel, out_shape=(jax.ShapeDtypeStruct((CELLS, C),...  71.5 us
    pallas_call x1, Pallas kernels, hand_over(): pl.pallas_call(hand_kernel, out_shape=(jax.ShapeDtypeStruct((CELLS, C), B...  2.19 us

profile of v2, /device:TPU:1, one launch (start us, length us, event | category | flops | bytes accessed | tf_op | source)
XLA Modules:
  0.0 74.5 jit_solution(15724137560967669930)
XLA Ops:
  0.6 71.5 %window.1 = (bf16[1024,256]{1,0:T(8,128)(2,1)}, bf16[2048,256]{1,0:T(8,128)(2,1)}) custom-call(bf16[2,4,128,256]{3,2,1,0:T(8,128)(2,1)} %lat_hbm.1, bf16[3,3,3,256,256]{4,3,2,1,0:T(8,128)(2,1)} %w1_ref.1, bf16[3,3,3,256,256]{4,3,2,1,0:T(8,128)(2,1)} %w2_ref.1, bf16[32768,256]{1,0:T(8,128)(2,1)} %book_ref.1, s32[8,128]{1,0:T(8,128)} %bitcast.4, ...), custom_call_target="tpu_custom_call" | custom-call | tf_op jit(solution)/shard_map/window/pallas_call | solution.py:510
  72.1 2.2 %hand_over.1 = (bf16[1024,256]{1,0:T(8,128)(2,1)}, bf16[2048,256]{1,0:T(8,128)(2,1)}) custom-call(bf16[1024,256]{1,0:T(8,128)(2,1)} %get-tuple-element.6.grad_in, bf16[2048,256]{1,0:T(8,128)(2,1)} %get-tuple-element.7.sums_in), custom_call_target="tpu_custom_call" | custom-call | tf_op jit(solution)/shard_map/hand_over/pallas_call | solution.py:587

commit v3 on v2

--- a/solution.py
+++ b/solution.py
@@ -1,4 +1,4 @@
-import functools
+import contextlib
 
 import jax
 import jax.numpy as jnp
@@ -19,6 +19,11 @@
 K_OWN = 2048
 CELLS = 1024
 VMEM_LIMIT = 60 * 1024 * 1024
+STEPS = ((2, 0), (2, 1), (1, 0), (1, 1), (3, 0), (3, 1), (0, 1), (0, 0))
+
+
+def scope(name):
+    return contextlib.nullcontext()
 
 
 def onehot(cond):
@@ -40,6 +45,11 @@
     turned = upward - summed * (jnp.sum(summed * upward, -1, keepdims=True) / (1.0 + cosine))
     turned = turned + 2.0 * lat_unit * jnp.sum(quant_unit * upward, -1, keepdims=True)
     return quant_norm / lat_norm * turned + 0.5 * (latent - quant)
+
+
+def masked(low, high):
+    tiles = low.reshape(low.shape[0] // 16, 16, 128)
+    return (tiles * jnp.broadcast_to(high, (16, 128)).astype(BF16)[None]).reshape(low.shape)
 
 
 def column(row):
@@ -127,6 +137,9 @@
                     w_sem.at[c, p],
                 ).start()
 
+    for p in (2, 1, 0):
+        weights_start(0, p)
+
     def weights_here(c, p):
         pltpu.make_async_copy(wv.at[c, p], wv.at[c, p], w_sem.at[c, p]).wait()
 
@@ -157,11 +170,16 @@
             device_id_type=MESH,
         )
 
+    def column_at(i, sign):
+        dx, dc = STEPS[i]
+        x = lax.rem(lax.div(h, 2) + 4 + sign * dx, 4)
+        return x * 2 + lax.rem(lax.rem(h, 2) + dc, 2)
+
     def code_copy(i):
-        to = at_h(i)
+        to = column_at(i, 1)
         return pltpu.make_async_remote_copy(
             src_ref=msg.at[pl.ds(pl.multiple_of(to * NT, NT), NT)],
-            dst_ref=rcodes.at[h],
+            dst_ref=rcodes.at[:, h],
             send_sem=cs_sem.at[i],
             recv_sem=cr_sem.at[i],
             device_id=(t, to),
@@ -169,7 +187,7 @@
         )
 
     def row_copy(i, s):
-        to = at_h(i)
+        to = column_at(i, 1)
         return pltpu.make_async_remote_copy(
             src_ref=sbuf.at[to, pl.ds(s * 64, 64)],
             dst_ref=rbuf.at[h, pl.ds(s * 64, 64)],
@@ -179,28 +197,29 @@
             device_id_type=MESH,
         )
 
-    def owner(i, dt):
-        to_t, to_h = lax.rem(t + dt, NT), at_h(i)
-        return to_t, to_h, to_h * NT + to_t
-
-    def key_copy(i, dt):
-        to_t, to_h, blk = owner(i, dt)
+    def key_copy(dt):
+        to = lax.rem(t + dt, NT)
         return pltpu.make_async_remote_copy(
-            src_ref=msg.at[blk],
-            dst_ref=crecv.at[i * NT + t],
-            send_sem=ks_sem,
-            recv_sem=kr_sem,
-            device_id=(to_t, to_h),
+            src_ref=rcodes.at[to],
+            dst_ref=crecv.at[:, t],
+            send_sem=ks_sem.at[dt],
+            recv_sem=kr_sem.at[dt],
+            device_id=(to, h),
             device_id_type=MESH,
         )
 
-    def term_copy(i, dt):
-        to_t, to_h, blk = owner(i, dt)
+    def term_copy(i, k):
+        def far(n):
+            return lax.rem(2 + 3 * n + lax.div(n, 2) * (3 + 2 * lax.rem(n, 2)), 4)
+
+        y = lax.rem(lax.rem(t, 4) + far(lax.rem(k, 4)), 4)
+        z = lax.rem(lax.div(t, 4) + far(lax.div(k, 4)), 4)
+        to_t, to_h = z * 4 + y, column_at(i, 1)
         return pltpu.make_async_remote_copy(
-            src_ref=tsend.at[pl.ds(pl.multiple_of(blk * CAP, CAP), CAP)],
+            src_ref=tsend.at[pl.ds(pl.multiple_of((to_h * NT + to_t) * CAP, CAP), CAP)],
             dst_ref=trecv.at[pl.ds(pl.multiple_of((i * NT + t) * CAP, CAP), CAP)],
             send_sem=gs_sem,
-            recv_sem=gr_sem.at[i // 4],
+            recv_sem=gr_sem.at[i // 2],
             device_id=(to_t, to_h),
             device_id_type=MESH,
         )
@@ -240,7 +259,6 @@
             t_copy(c, f, part).start()
 
     lane_i = lax.broadcasted_iota(I32, (128, 128), 1)
-    lanes = lane_i.astype(F32)
 
     def make_slots():
         codes = codes_ref[...]
@@ -270,22 +288,24 @@
         m_lo = jnp.dot(ht, jnp.concatenate(v_lo, 0), preferred_element_type=F32)
         msg[...] = (m_hi * 64.0 + m_lo).astype(I32)
 
-    def asked_rows():
-        for i in range(1, NH):
-            code_copy(i).wait_recv()
-        lane_src = lax.shift_right_logical(lax.broadcasted_iota(I32, (NT, 128), 1), 4)
-        rowmat = jnp.zeros((NT, 128), I32)
-        for s in range(NH):
-            rowmat = rowmat + jnp.where(lane_src == s, rcodes[s], 0)
-        return rowmat.astype(F32) - 1.0
-
-    def gather(rowmat, k):
+    group8 = lax.broadcasted_iota(I32, (8, 128), 0)
+    mine = lax.shift_right_logical(lax.broadcasted_iota(I32, (8, 128), 1), 4) == group8
+
+    def key_row(tile):
+        return jnp.sum(jnp.where(mine, tile, 0), axis=0, keepdims=True) - 1
+
+    def pick_rows(want, tiles):
+        want = want.astype(I32)
+        low = onehot(jnp.bitwise_and(want, 127) == lane_i)
+        high = lax.shift_right_arithmetic(want, 7).astype(F32).astype(BF16)
+        return jnp.concatenate(
+            [jnp.where(high == float(j), low, jnp.zeros_like(low)) for j in range(tiles)], 1
+        )
+
+    def gather(k):
         for g in range(4 * k, 4 * k + 4):
             book_copy(g).wait()
-            want = column(rowmat[g : g + 1, :])
-            pick = jnp.concatenate(
-                [onehot(want - 128.0 * j == lanes) for j in range(K_OWN // 128)], 1
-            )
+            pick = pick_rows(column(key_row(rcodes[g]).astype(F32)), K_OWN // 128)
             found = jnp.dot(pick, cbuf[g % 4], preferred_element_type=F32).astype(BF16)
             for s in range(NH):
                 sbuf[s, pl.ds(g * CAP, CAP)] = found[s * CAP : (s + 1) * CAP]
@@ -293,7 +313,7 @@
                 book_copy(g + 4).start()
 
     def send_rows(k):
-        for i in range(1, NH):
+        for i in range(NH - 1):
             row_copy(i, k).start()
 
     def tell(r, by):
@@ -304,189 +324,215 @@
 
     lane = lax.broadcasted_iota(I32, (256, 128), 0)
 
+    def lay_one_hot(ref, lanes_at, row):
+        low = onehot(lane == jnp.broadcast_to(jnp.bitwise_and(row, 255), (256, 128)))
+        high = lax.shift_right_arithmetic(row, 8)
+        for b in range(8):
+            ref[pl.ds(b * 256, 256), lanes_at] = masked(low, jnp.where(high == b, 1.0, 0.0))
+
     def make_place():
-        @pl.loop(0, SLOTS // 256)
-        def _(b):
-            rows = pl.ds(pl.multiple_of(b * 256, 256), 256)
-            for j in range(8):
-                row = slot[pl.ds(j, 1), :] - b * 256
-                place[j // 4, rows, pl.ds((j % 4) * 128, 128)] = onehot(
-                    lane == jnp.broadcast_to(row, (256, 128))
-                )
+        for j in range(8):
+            lay_one_hot(place.at[j // 4], pl.ds((j % 4) * 128, 128), slot[pl.ds(j, 1), :])
 
     def make_spread():
-        pltpu.make_async_copy(crecv, crecv, kr_sem).wait()
-        group = lax.broadcasted_iota(I32, (8, 128), 0)
-        mine = lax.shift_right_logical(lax.broadcasted_iota(I32, (8, 128), 1), 4) == group
-        row_of = []
-        for j in range(SLOTS // 128):
-            tile = crecv[pl.ds(j * 8, 8)]
-            row_of.append(jnp.sum(jnp.where(mine, tile, 0), axis=0, keepdims=True) - 1)
-
-        @pl.loop(0, K_OWN // 256)
-        def _(b):
-            rows = pl.ds(pl.multiple_of(b * 256, 256), 256)
-            for j in range(SLOTS // 128):
-                spread_in[rows, pl.ds(j * 128, 128)] = onehot(
-                    lane == jnp.broadcast_to(row_of[j] - b * 256, (256, 128))
-                )
+        for dt in range(1, NT):
+            key_copy(dt).wait_recv()
+        own_keys.wait()
+        for i in range(NH):
+            keys = crecv[column_at(i, -1)]
+            for half in range(2):
+                row = key_row(keys[half * 8 : half * 8 + 8])
+                lay_one_hot(spread_in, pl.ds(i * 256 + half * 128, 128), row)
+
+    def next_frame(f):
+        with scope("next"):
+            for i in range(4):
+                x = finish(f, i, lat[f, i])
+                first[f, i] = x
+                ext[1, 2 + f, 1 + i] = norm_act(x.astype(F32))
+        send_frame(1, f)
+
+    def rows_of(c, e):
+        with scope("wait_x"):
+            for d in range(2):
+                x_copy(c, e, d).wait_recv()
+        with scope("widen"):
+            widen(c, e)
+
+    def forward(c, e):
+        with scope(f"wait_edge{c}{e}"):
+            for d in range(2):
+                t_copy(c, e, d).wait_recv()
+                x_copy(c, e, d).start()
+
+    def earlier_frame(c, e):
+        with scope(f"wait_mid{c}{e}"):
+            t_copy(c, e, 2).wait_recv()
+        with scope(f"wait_fwd{c}{e}"):
+            for d in range(2):
+                x_copy(c, e, d).wait_recv()
 
     for f in (1, 0):
-        lat_in[f].wait()
-        for i in range(4):
-            ext[0, 2 + f, 1 + i] = norm_act(lat[f, i].astype(F32))
+        with scope("latin"):
+            lat_in[f].wait()
+        with scope("act"):
+            for i in range(4):
+                ext[0, 2 + f, 1 + i] = norm_act(lat[f, i].astype(F32))
         if f == 1:
-            pl.semaphore_wait(barrier, NH + 1)
+            with scope("barrier"):
+                pl.semaphore_wait(barrier, NH + 1)
         send_frame(0, f)
     tell(0, 1)
-    for c in range(2):
-        for p in (2, 1, 0):
-            weights_start(c, p)
-        if c == 0:
-            for g in range(4):
-                book_copy(g).start()
+    for g in range(4):
+        book_copy(g).start()
     up_in.start()
 
-    make_slots()
-    for i in range(1, NH):
+    with scope("slots"):
+        make_slots()
+    for i in range(NH - 1):
         code_copy(i).start()
-    rcodes[h] = msg[pl.ds(pl.multiple_of(h * NT, NT), NT)]
-
-    def local_part(c):
-        for e in (3, 2):
-            for d in range(2):
-                x_copy(c, e, d).wait_recv()
-            widen(c, e)
-        if c == 1:
-            send_rows(2)
-        weights_here(c, 2)
-        weights_here(c, 1)
-        acc[1] = product(c, 3, 2)
-        acc[1] += product(c, 2, 1)
-        acc[0] = product(c, 2, 2)
-
-    def earlier_frame(c, e, between, rows_piece):
-        for d in range(2):
-            t_copy(c, e, d).wait_recv()
-            x_copy(c, e, d).start()
-        if between is not None:
-            between()
-        t_copy(c, e, 2).wait_recv()
-        for d in range(2):
-            x_copy(c, e, d).wait_recv()
-        if rows_piece is not None:
-            send_rows(rows_piece)
-        widen(c, e)
-        if e == 1:
-            weights_here(c, 0)
-            acc[1] += product(c, 1, 0)
-        else:
-            acc[0] += product(c, 0, 0)
-
-    def next_frame(f):
-        for i in range(4):
-            x = finish(f, i, lat[f, i])
-            first[f, i] = x
-            ext[1, 2 + f, 1 + i] = norm_act(x.astype(F32))
-        send_frame(1, f)
-
-    local_part(0)
-    rowmat = asked_rows()
-    gather(rowmat, 0)
-    gather(rowmat, 1)
-    pl.semaphore_wait(know.at[0], 2)
+    rcodes[:, h] = msg[pl.ds(pl.multiple_of(h * NT, NT), NT)]
+
+    rows_of(0, 3)
+    weights_here(0, 2)
+    with scope("mm"):
+        acc[1] = product(0, 3, 2)
+    rows_of(0, 2)
+    forward(0, 1)
+    weights_here(0, 1)
+    with scope("mm"):
+        acc[1] += product(0, 2, 1)
+        acc[0] = product(0, 2, 2)
+    for p in (2, 1, 0):
+        weights_start(1, p)
+    with scope("asked"):
+        for i in range(NH - 1):
+            code_copy(i).wait_recv()
+    with scope("gather"):
+        gather(0)
+    with scope("know"):
+        pl.semaphore_wait(know.at[0], 2)
     tell(1, 2)
-    earlier_frame(0, 1, lambda: gather(rowmat, 2), 0)
+    earlier_frame(0, 1)
+    send_rows(0)
+    weights_here(0, 0)
+    with scope("mm"):
+        widen(0, 1)
+        acc[1] += product(0, 1, 0)
     next_frame(1)
-    acc[0] += product(0, 1, 1)
-    pl.semaphore_wait(know.at[1], 2)
+    with scope("mm"):
+        acc[0] += product(0, 1, 1)
+    forward(0, 0)
+    with scope("know"):
+        pl.semaphore_wait(know.at[1], 2)
     tell(2, 4)
-    gather(rowmat, 3)
-    rbuf[h] = sbuf[h]
-    earlier_frame(0, 0, None, 1)
+    with scope("gather"):
+        gather(1)
+        gather(2)
+    earlier_frame(0, 0)
+    send_rows(1)
+    with scope("mm"):
+        widen(0, 0)
+        acc[0] += product(0, 0, 0)
     next_frame(0)
 
-    pl.semaphore_wait(know.at[2], 2)
+    with scope("know"):
+        pl.semaphore_wait(know.at[2], 2)
     for i in range(1, NH):
         pl.semaphore_signal(know.at[3], inc=1, device_id=(t, at_h(i)), device_id_type=MESH)
-    make_place()
-    local_part(1)
-
-    def send_keys():
-        pl.semaphore_wait(know.at[3], NH - 1)
-        for i in range(NH):
-
-            @pl.loop(1 if i == 0 else 0, NT)
-            def _(dt):
-                key_copy(i, dt).start()
-
-        pltpu.make_async_copy(msg.at[h * NT + t], crecv.at[t], kr_sem).start()
-
-    send_keys()
-    earlier_frame(1, 1, None, 3)
+    for dt in range(1, NT):
+        key_copy(dt).start()
+    own_keys = pltpu.make_async_copy(rcodes.at[t], crecv.at[:, t], kr_sem.at[0])
+    own_keys.start()
+    rows_of(1, 3)
+    weights_here(1, 2)
+    with scope("mm"):
+        acc[1] = product(1, 3, 2)
+    forward(1, 1)
+    with scope("gather"):
+        gather(3)
+    rbuf[h] = sbuf[h]
+    with scope("place"):
+        make_place()
+    rows_of(1, 2)
+    send_rows(2)
+    weights_here(1, 1)
+    with scope("mm"):
+        acc[1] += product(1, 2, 1)
+        acc[0] = product(1, 2, 2)
+    earlier_frame(1, 1)
+    send_rows(3)
+    weights_here(1, 0)
+    with scope("mm"):
+        widen(1, 1)
+        acc[1] += product(1, 1, 0)
     for i in range(4):
         enc[1, pl.ds(i * 128, 128)] = finish(1, i, first[1, i])
-    acc[0] += product(1, 1, 1)
-    placed[...] = jnp.dot(place[1], enc[1], preferred_element_type=F32)
-    make_spread()
-    earlier_frame(1, 0, None, None)
+    with scope("mm"):
+        acc[0] += product(1, 1, 1)
+    forward(1, 0)
+    with scope("placed"):
+        placed[...] = jnp.dot(place[1], enc[1], preferred_element_type=F32)
+    with scope("spread"):
+        make_spread()
+    with scope("know"):
+        pl.semaphore_wait(know.at[3], NH - 1)
+    earlier_frame(1, 0)
+    with scope("mm"):
+        widen(1, 0)
+        acc[0] += product(1, 0, 0)
     for i in range(4):
         enc[0, pl.ds(i * 128, 128)] = finish(0, i, first[0, i])
 
-    for s in range(4):
-        for i in range(1, NH):
-            row_copy(i, s).wait_recv()
-
-    for i in range(NH):
-        to_h = at_h(i)
-        rows = pl.ds(pl.multiple_of(to_h * 256, 256), 256)
-        total = placed[rows] + jnp.dot(place[0, rows], enc[0], preferred_element_type=F32)
-        tsend[rows] = (rbuf[to_h].astype(F32) - total).astype(BF16)
-
-        @pl.loop(1 if i == 0 else 0, NT)
-        def _(dt):
-            term_copy(i, dt).start()
-
-        if i == 0:
-            pltpu.make_async_copy(
-                tsend.at[pl.ds(pl.multiple_of((h * NT + t) * CAP, CAP), CAP)],
-                trecv.at[pl.ds(pl.multiple_of(t * CAP, CAP), CAP)],
-                gr_sem.at[0],
-            ).start()
-
-    up_in.wait()
-    rows_all = rbuf[...].reshape(SLOTS, C)
-    for j in range(8):
-        want = column(slot[pl.ds(j, 1), :].astype(F32))
-        pick = jnp.concatenate([onehot(want - 128.0 * k == lanes) for k in range(SLOTS // 128)], 1)
-        quant = jnp.dot(pick, rows_all, preferred_element_type=F32)
-        cells = pl.ds((j % 4) * 128, 128)
-        grad_out[pl.ds(j * 128, 128)] = rotate_back(
-            enc[j // 4, cells].astype(F32), quant, up[pl.ds(j * 128, 128)].astype(F32)
-        ).astype(BF16)
+    with scope("wait_rows"):
+        for s in range(4):
+            for i in range(NH - 1):
+                row_copy(i, s).wait_recv()
+
+    for chip in range(4):
+        to_x = lax.rem(lax.div(h, 2) + STEPS[2 * chip][0], 4)
+        rows = pl.ds(pl.multiple_of(to_x * 512, 512), 512)
+        with scope("terms"):
+            total = placed[rows] + jnp.dot(place[0, rows], enc[0], preferred_element_type=F32)
+            pair = rbuf[pl.ds(to_x * 2, 2)].reshape(512, C)
+            tsend[rows] = (pair.astype(F32) - total).astype(BF16)
+
+        @pl.loop(0, NT)
+        def _(k):
+            term_copy(2 * chip, k).start()
+            if chip < 3:
+                term_copy(2 * chip + 1, k).start()
+            else:
+
+                @pl.when(k < NT - 1)
+                def _():
+                    term_copy(NH - 1, k).start()
+
+    pltpu.make_async_copy(
+        tsend.at[pl.ds(pl.multiple_of((h * NT + t) * CAP, CAP), CAP)],
+        trecv.at[pl.ds(pl.multiple_of(((NH - 1) * NT + t) * CAP, CAP), CAP)],
+        gr_sem.at[3],
+    ).start()
+
+    with scope("grad"):
+        up_in.wait()
+        rows_all = rbuf[...].reshape(SLOTS, C)
+        for j in range(8):
+            pick = pick_rows(column(slot[pl.ds(j, 1), :].astype(F32)), SLOTS // 128)
+            quant = jnp.dot(pick, rows_all, preferred_element_type=F32)
+            cells = pl.ds((j % 4) * 128, 128)
+            grad_out[pl.ds(j * 128, 128)] = rotate_back(
+                enc[j // 4, cells].astype(F32), quant, up[pl.ds(j * 128, 128)].astype(F32)
+            ).astype(BF16)
     grad_done = pltpu.make_async_copy(grad_out, grad_hbm, out_sem.at[0])
     grad_done.start()
 
-    half = SLOTS // 2
-    low, high = pl.ds(0, half), pl.ds(half, half)
-    pltpu.make_async_copy(trecv.at[low], trecv.at[low], gr_sem.at[0]).wait()
-    sums[...] = jnp.dot(spread_in[:, low], trecv[low], preferred_element_type=F32)
-    pltpu.make_async_copy(trecv.at[high], trecv.at[high], gr_sem.at[1]).wait()
-    done = []
-    for b in range(4):
-        rows = pl.ds(b * 512, 512)
-        total = sums[rows] + jnp.dot(
-            spread_in[rows, high], trecv[high], preferred_element_type=F32
-        )
-        sums_out[rows] = (2.0 * total).astype(BF16)
-        copy = pltpu.make_async_copy(sums_out.at[rows], sums_hbm.at[rows], out_sem.at[1 + b])
-        copy.start()
-        done.append(copy)
-
-    for i in range(1, NH):
+    for i in range(NH - 1):
         code_copy(i).wait_send()
         for s in range(4):
             row_copy(i, s).wait_send()
+    for dt in range(1, NT):
+        key_copy(dt).wait_send()
     for c in range(2):
         for e in range(4):
             for d in range(2):
@@ -494,10 +540,36 @@
         for e in range(2):
             for part in range(3):
                 t_copy(c, e, part).wait_send()
+
+    def arrived(chip):
+        part = pl.ds(chip * 512, 512)
+        with scope(f"wait_terms{chip}"):
+            pltpu.make_async_copy(trecv.at[part], trecv.at[part], gr_sem.at[chip]).wait()
+
+    def summed(rows, part):
+        return jnp.dot(spread_in[rows, part], trecv[part], preferred_element_type=F32)
+
+    everything = pl.ds(0, K_OWN)
+    arrived(0)
+    arrived(1)
+    with scope("sums"):
+        sums[...] = summed(everything, pl.ds(0, 1024))
+    arrived(2)
+    with scope("sums"):
+        sums[...] += summed(everything, pl.ds(1024, 512))
     sent = pl.ds(0, SLOTS - CAP)
-    pltpu.make_async_copy(tsend.at[sent], tsend.at[sent], gs_sem).wait()
-    sent = pl.ds(0, OWN - 1)
-    pltpu.make_async_copy(crecv.at[sent], crecv.at[sent], ks_sem).wait()
+    with scope("sent"):
+        pltpu.make_async_copy(tsend.at[sent], tsend.at[sent], gs_sem).wait()
+    arrived(3)
+    done = []
+    with scope("sums"):
+        for b in range(2):
+            rows = pl.ds(b * 1024, 1024)
+            total = sums[rows] + summed(rows, pl.ds(1536, 512))
+            sums_out[rows] = (2.0 * total).astype(BF16)
+            copy = pltpu.make_async_copy(sums_out.at[rows], sums_hbm.at[rows], out_sem.at[1 + b])
+            copy.start()
+            done.append(copy)
     grad_done.wait()
     for copy in done:
         copy.wait()
@@ -526,7 +598,7 @@
             pltpu.VMEM((2, 512, C), BF16),
             pltpu.VMEM((OWN, 128), I32),
             pltpu.VMEM((8, 128), I32),
-            pltpu.VMEM((NH, NT, 128), I32),
+            pltpu.VMEM((NT, NH, 128), I32),
             pltpu.VMEM((4, K_OWN, C), BF16),
             pltpu.VMEM((NH, 256, C), BF16),
             pltpu.VMEM((NH, 256, C), BF16),
@@ -534,7 +606,7 @@
             pltpu.VMEM((SLOTS, C), F32),
             pltpu.VMEM((SLOTS, C), BF16),
             pltpu.VMEM((SLOTS, C), BF16),
-            pltpu.VMEM((OWN, 128), I32),
+            pltpu.VMEM((NH, NT, 128), I32),
             pltpu.VMEM((K_OWN, SLOTS), BF16),
             pltpu.VMEM((K_OWN, C), F32),
             pltpu.VMEM((K_OWN, C), BF16),
@@ -550,11 +622,11 @@
             dma((4,)),
             dma((NH, 4)),
             dma((NH, 4)),
+            dma((NT,)),
+            dma((NT,)),
             dma,
-            dma,
-            dma,
-            dma((2,)),
-            dma((5,)),
+            dma((4,)),
+            dma((3,)),
             pltpu.SemaphoreType.REGULAR((4,)),
         ],
         compiler_params=pltpu.CompilerParams(

time: 74.7 us -> 63.7 us (0.85)
  Pallas kernels: 73.7 us -> 62.7 us
    pallas_call x1, Pallas kernels: 71.5 us -> 60.5 us  [window(): pl.pallas_call(window_kernel, out_shape=(jax.ShapeDtypeStruct((CELLS, C),...]
where the time goes in v3:
time: 63.7 us; the launch traced here: 63.5 us
  Pallas kernels  62.7 us (98%)
  between operations  0.8 us (1%)
    pallas_call x1, Pallas kernels, window(): pl.pallas_call(window_kernel, out_shape=(jax.ShapeDtypeStruct((CELLS, C),...  60.5 us
    pallas_call x1, Pallas kernels, hand_over(): pl.pallas_call(hand_kernel, out_shape=(jax.ShapeDtypeStruct((CELLS, C), B...  2.19 us

profile of v3, /device:TPU:1, one launch (start us, length us, event | category | flops | bytes accessed | tf_op | source)
XLA Modules:
  0.0 63.5 jit_solution(16753413707826724977)
XLA Ops:
  0.6 60.5 %window.1 = (bf16[1024,256]{1,0:T(8,128)(2,1)}, bf16[2048,256]{1,0:T(8,128)(2,1)}) custom-call(bf16[2,4,128,256]{3,2,1,0:T(8,128)(2,1)} %lat_hbm.1, bf16[3,3,3,256,256]{4,3,2,1,0:T(8,128)(2,1)} %w1_ref.1, bf16[3,3,3,256,256]{4,3,2,1,0:T(8,128)(2,1)} %w2_ref.1, bf16[32768,256]{1,0:T(8,128)(2,1)} %book_ref.1, s32[8,128]{1,0:T(8,128)} %bitcast.4, ...), custom_call_target="tpu_custom_call" | custom-call | tf_op jit(solution)/shard_map/window/pallas_call | solution.py:582
  61.2 2.2 %hand_over.1 = (bf16[1024,256]{1,0:T(8,128)(2,1)}, bf16[2048,256]{1,0:T(8,128)(2,1)}) custom-call(bf16[1024,256]{1,0:T(8,128)(2,1)} %get-tuple-element.6.grad_in, bf16[2048,256]{1,0:T(8,128)(2,1)} %get-tuple-element.7.sums_in), custom_call_target="tpu_custom_call" | custom-call | tf_op jit(solution)/shard_map/hand_over/pallas_call | solution.py:659

commit v4 on v3

--- a/solution.py
+++ b/solution.py
@@ -110,17 +110,28 @@
     h = lax.axis_index("height")
     h_up, h_down = lax.rem(h + NH - 1, NH), lax.rem(h + 1, NH)
 
-    def at_t(by):
-        return lax.rem(t + NT + by, NT)
-
     def at_h(by):
         return lax.rem(h + by, NH)
 
     barrier = pltpu.get_barrier_semaphore()
+
+    def if_in(by):
+        return pl.when(t + by < NT) if by > 0 else pl.when(t + by >= 0)
+
     for by in (1, -1):
-        pl.semaphore_signal(barrier, inc=1, device_id=(at_t(by), h), device_id_type=MESH)
+
+        @if_in(by)
+        def _():
+            pl.semaphore_signal(barrier, inc=1, device_id=(t + by, h), device_id_type=MESH)
+
     for i in range(1, NH):
         pl.semaphore_signal(barrier, inc=1, device_id=(t, at_h(i)), device_id_type=MESH)
+
+    def places(by):
+        return lax.div(t + NT - by, NT) + lax.div(2 * NT - 1 - t - by, NT)
+
+    def all_entered():
+        pl.semaphore_wait(barrier, NH - 1 + places(1))
 
     lat_in = [pltpu.make_async_copy(lat_hbm.at[f], lat.at[f], in_sem.at[f]) for f in range(2)]
     up_in = pltpu.make_async_copy(up_hbm, up, in_sem.at[2])
@@ -137,15 +148,12 @@
                     w_sem.at[c, p],
                 ).start()
 
-    for p in (2, 1, 0):
-        weights_start(0, p)
-
     def weights_here(c, p):
         pltpu.make_async_copy(wv.at[c, p], wv.at[c, p], w_sem.at[c, p]).wait()
 
     def book_copy(g):
         return pltpu.make_async_copy(
-            book_ref.at[pl.ds(g * K_OWN, K_OWN)], cbuf.at[g % 4], cb_sem.at[g % 4]
+            book_ref.at[pl.ds(g * K_OWN, K_OWN)], cbuf.at[g % 8], cb_sem.at[g % 8]
         )
 
     def x_copy(c, e, d):
@@ -166,9 +174,27 @@
             dst_ref=ext.at[c, e, rows],
             send_sem=ts_sem.at[c, e, part],
             recv_sem=tr_sem.at[c, e, part],
-            device_id=(at_t(1), h),
+            device_id=(lax.rem(t + 1, NT), h),
             device_id_type=MESH,
         )
+
+    def gives_x(d):
+        return h > 0 if d == 0 else h < NH - 1
+
+    def takes_x(d):
+        return h < NH - 1 if d == 0 else h > 0
+
+    def x_start(c, e, d):
+        @pl.when(gives_x(d))
+        def _():
+            x_copy(c, e, d).start()
+
+    def x_arrived(c, e):
+        for d in range(2):
+
+            @pl.when(takes_x(d))
+            def _():
+                x_copy(c, e, d).wait_recv()
 
     def column_at(i, sign):
         dx, dc = STEPS[i]
@@ -186,13 +212,13 @@
             device_id_type=MESH,
         )
 
-    def row_copy(i, s):
+    def row_copy(i, g):
         to = column_at(i, 1)
         return pltpu.make_async_remote_copy(
-            src_ref=sbuf.at[to, pl.ds(s * 64, 64)],
-            dst_ref=rbuf.at[h, pl.ds(s * 64, 64)],
-            send_sem=rs_sem.at[i, s],
-            recv_sem=rr_sem.at[i, s],
+            src_ref=sbuf.at[to, pl.ds(g * CAP, CAP)],
+            dst_ref=rbuf.at[h, pl.ds(g * CAP, CAP)],
+            send_sem=rs_sem.at[i],
+            recv_sem=rr_sem.at[i],
             device_id=(t, to),
             device_id_type=MESH,
         )
@@ -239,8 +265,12 @@
                     x = jnp.where(ok, x, jnp.zeros_like(x))
                 cat[e, pl.ds(i * 128, 128), pl.ds(q * C, C)] = x
 
-    def product(c, e, p):
-        return jnp.dot(cat[e], wv[c, p], preferred_element_type=F32)
+    def product(f, c, e, p, fresh=False):
+        for m in range(2):
+            for n in range(3):
+                rows, cols = pl.ds(m * 256, 256), pl.ds(n * C, C)
+                part = jnp.dot(cat[e, rows], wv[c, p, :, cols], preferred_element_type=F32)
+                acc[f, rows, cols] = part if fresh else acc[f, rows, cols] + part
 
     col = lax.broadcasted_iota(I32, (128, C), 0)
 
@@ -254,9 +284,12 @@
 
     def send_frame(c, f):
         for d in range(2):
-            x_copy(c, 2 + f, d).start()
-        for part in range(3):
-            t_copy(c, f, part).start()
+            x_start(c, 2 + f, d)
+
+        @pl.when(t < NT - 1)
+        def _():
+            for part in range(3):
+                t_copy(c, f, part).start()
 
     lane_i = lax.broadcasted_iota(I32, (128, 128), 1)
 
@@ -303,24 +336,37 @@
         )
 
     def gather(k):
-        for g in range(4 * k, 4 * k + 4):
+        group = range(4 * k, 4 * k + 4)
+        for g in group:
             book_copy(g).wait()
-            pick = pick_rows(column(key_row(rcodes[g]).astype(F32)), K_OWN // 128)
-            found = jnp.dot(pick, cbuf[g % 4], preferred_element_type=F32).astype(BF16)
+        picks = [
+            pick_rows(column(key_row(rcodes[g]).astype(F32)), K_OWN // 128) for g in group
+        ]
+        for g, pick in zip(group, picks):
+            found = jnp.dot(pick, cbuf[g % 8], preferred_element_type=F32).astype(BF16)
             for s in range(NH):
                 sbuf[s, pl.ds(g * CAP, CAP)] = found[s * CAP : (s + 1) * CAP]
-            if g + 4 < NT:
-                book_copy(g + 4).start()
-
-    def send_rows(k):
-        for i in range(NH - 1):
-            row_copy(i, k).start()
-
-    def tell(r, by):
-        for sign in (1, -1):
-            pl.semaphore_signal(
-                know.at[r], inc=1, device_id=(at_t(sign * by), h), device_id_type=MESH
-            )
+        for g in group:
+            if g + 8 < NT:
+                book_copy(g + 8).start()
+
+    def send_rows(*ranges):
+        for g in ranges:
+            for i in range(NH - 1):
+                row_copy(i, g).start()
+
+    def all_rows(i, sem):
+        return pltpu.make_async_copy(rbuf.at[i], rbuf.at[i], sem.at[i])
+
+    def tell(r):
+        for by in (2**r, -(2**r)):
+
+            @if_in(by)
+            def _():
+                pl.semaphore_signal(know.at[r], inc=1, device_id=(t + by, h), device_id_type=MESH)
+
+    def told(r):
+        pl.semaphore_wait(know.at[r], places(2**r))
 
     lane = lax.broadcasted_iota(I32, (256, 128), 0)
 
@@ -332,7 +378,7 @@
 
     def make_place():
         for j in range(8):
-            lay_one_hot(place.at[j // 4], pl.ds((j % 4) * 128, 128), slot[pl.ds(j, 1), :])
+            lay_one_hot(place, pl.ds(j * 128, 128), slot[pl.ds(j, 1), :])
 
     def make_spread():
         for dt in range(1, NT):
@@ -354,24 +400,37 @@
 
     def rows_of(c, e):
         with scope("wait_x"):
-            for d in range(2):
-                x_copy(c, e, d).wait_recv()
+            x_arrived(c, e)
         with scope("widen"):
             widen(c, e)
 
     def forward(c, e):
         with scope(f"wait_edge{c}{e}"):
-            for d in range(2):
-                t_copy(c, e, d).wait_recv()
-                x_copy(c, e, d).start()
+
+            @pl.when(t > 0)
+            def _():
+                for d in range(2):
+                    t_copy(c, e, d).wait_recv()
+                    x_start(c, e, d)
 
     def earlier_frame(c, e):
-        with scope(f"wait_mid{c}{e}"):
-            t_copy(c, e, 2).wait_recv()
-        with scope(f"wait_fwd{c}{e}"):
-            for d in range(2):
-                x_copy(c, e, d).wait_recv()
-
+        @pl.when(t > 0)
+        def _():
+            with scope(f"wait_mid{c}{e}"):
+                t_copy(c, e, 2).wait_recv()
+            with scope(f"wait_fwd{c}{e}"):
+                x_arrived(c, e)
+
+    def mm(*args, **kw):
+        with scope("mm"):
+            product(*args, **kw)
+
+    def fetch(k):
+        with scope("gather"):
+            gather(k)
+
+    with scope("slots"):
+        make_slots()
     for f in (1, 0):
         with scope("latin"):
             lat_in[f].wait()
@@ -379,121 +438,128 @@
             for i in range(4):
                 ext[0, 2 + f, 1 + i] = norm_act(lat[f, i].astype(F32))
         if f == 1:
+            weights_start(0, 2)
             with scope("barrier"):
-                pl.semaphore_wait(barrier, NH + 1)
+                all_entered()
         send_frame(0, f)
-    tell(0, 1)
+        if f == 1:
+            for i in range(NH - 1):
+                code_copy(i).start()
+    tell(0)
     for g in range(4):
         book_copy(g).start()
-    up_in.start()
-
-    with scope("slots"):
-        make_slots()
-    for i in range(NH - 1):
-        code_copy(i).start()
+    weights_start(0, 1)
+    weights_start(0, 0)
     rcodes[:, h] = msg[pl.ds(pl.multiple_of(h * NT, NT), NT)]
-
-    rows_of(0, 3)
-    weights_here(0, 2)
-    with scope("mm"):
-        acc[1] = product(0, 3, 2)
-    rows_of(0, 2)
-    forward(0, 1)
-    weights_here(0, 1)
-    with scope("mm"):
-        acc[1] += product(0, 2, 1)
-        acc[0] = product(0, 2, 2)
-    for p in (2, 1, 0):
-        weights_start(1, p)
+    for g in range(4, 8):
+        book_copy(g).start()
+    with scope("place"):
+        make_place()
     with scope("asked"):
         for i in range(NH - 1):
             code_copy(i).wait_recv()
-    with scope("gather"):
-        gather(0)
+    fetch(0)
+    send_rows(0, 1)
+    rows_of(0, 3)
+    weights_here(0, 2)
+    mm(1, 0, 3, 2, fresh=True)
+    rows_of(0, 2)
+    forward(0, 1)
+    send_rows(2)
+    weights_here(0, 1)
+    mm(1, 0, 2, 1)
+    send_rows(3)
+    mm(0, 0, 2, 2, fresh=True)
+    for p in (2, 1, 0):
+        weights_start(1, p)
+    earlier_frame(0, 1)
+    weights_here(0, 0)
+    with scope("widen"):
+        widen(0, 1)
+    mm(1, 0, 1, 0)
+    next_frame(1)
+    fetch(1)
+    forward(0, 0)
+    send_rows(4)
+    mm(0, 0, 1, 1)
+    send_rows(5)
     with scope("know"):
-        pl.semaphore_wait(know.at[0], 2)
-    tell(1, 2)
-    earlier_frame(0, 1)
-    send_rows(0)
-    weights_here(0, 0)
-    with scope("mm"):
-        widen(0, 1)
-        acc[1] += product(0, 1, 0)
-    next_frame(1)
-    with scope("mm"):
-        acc[0] += product(0, 1, 1)
-    forward(0, 0)
+        told(0)
+    tell(1)
+    fetch(2)
+    send_rows(6)
+    earlier_frame(0, 0)
+    send_rows(7)
+    with scope("widen"):
+        widen(0, 0)
+    mm(0, 0, 0, 0)
+    next_frame(0)
+    send_rows(8)
     with scope("know"):
-        pl.semaphore_wait(know.at[1], 2)
-    tell(2, 4)
-    with scope("gather"):
-        gather(1)
-        gather(2)
-    earlier_frame(0, 0)
-    send_rows(1)
-    with scope("mm"):
-        widen(0, 0)
-        acc[0] += product(0, 0, 0)
-    next_frame(0)
-
+        told(1)
+    tell(2)
+    rows_of(1, 3)
+    weights_here(1, 2)
+    mm(1, 1, 3, 2, fresh=True)
+    forward(1, 1)
+    send_rows(9)
+    fetch(3)
+    rbuf[h] = sbuf[h]
+    up_in.start()
+    send_rows(10)
     with scope("know"):
-        pl.semaphore_wait(know.at[2], 2)
+        told(2)
+    tell(3)
+    rows_of(1, 2)
+    send_rows(11)
+    weights_here(1, 1)
+    mm(1, 1, 2, 1)
+    send_rows(12)
+    mm(0, 1, 2, 2, fresh=True)
+    earlier_frame(1, 1)
+    send_rows(13)
+    weights_here(1, 0)
+    with scope("widen"):
+        widen(1, 1)
+    mm(1, 1, 1, 0)
+    send_rows(14)
+    for i in range(4):
+        enc[pl.ds(512 + i * 128, 128)] = finish(1, i, first[1, i])
+    mm(0, 1, 1, 1)
+    forward(1, 0)
+    send_rows(15)
+    with scope("know"):
+        told(3)
     for i in range(1, NH):
-        pl.semaphore_signal(know.at[3], inc=1, device_id=(t, at_h(i)), device_id_type=MESH)
+        pl.semaphore_signal(know.at[4], inc=1, device_id=(t, at_h(i)), device_id_type=MESH)
     for dt in range(1, NT):
         key_copy(dt).start()
     own_keys = pltpu.make_async_copy(rcodes.at[t], crecv.at[:, t], kr_sem.at[0])
     own_keys.start()
-    rows_of(1, 3)
-    weights_here(1, 2)
-    with scope("mm"):
-        acc[1] = product(1, 3, 2)
-    forward(1, 1)
-    with scope("gather"):
-        gather(3)
-    rbuf[h] = sbuf[h]
-    with scope("place"):
-        make_place()
-    rows_of(1, 2)
-    send_rows(2)
-    weights_here(1, 1)
-    with scope("mm"):
-        acc[1] += product(1, 2, 1)
-        acc[0] = product(1, 2, 2)
-    earlier_frame(1, 1)
-    send_rows(3)
-    weights_here(1, 0)
-    with scope("mm"):
-        widen(1, 1)
-        acc[1] += product(1, 1, 0)
+    with scope("placed"):
+        for b in range(4):
+            rows = pl.ds(b * 512, 512)
+            placed[rows] = jnp.dot(place[rows, 512:], enc[512:], preferred_element_type=F32)
+    earlier_frame(1, 0)
+    with scope("widen"):
+        widen(1, 0)
+    mm(0, 1, 0, 0)
     for i in range(4):
-        enc[1, pl.ds(i * 128, 128)] = finish(1, i, first[1, i])
-    with scope("mm"):
-        acc[0] += product(1, 1, 1)
-    forward(1, 0)
-    with scope("placed"):
-        placed[...] = jnp.dot(place[1], enc[1], preferred_element_type=F32)
-    with scope("spread"):
-        make_spread()
+        enc[pl.ds(i * 128, 128)] = finish(0, i, first[0, i])
     with scope("know"):
-        pl.semaphore_wait(know.at[3], NH - 1)
-    earlier_frame(1, 0)
-    with scope("mm"):
-        widen(1, 0)
-        acc[0] += product(1, 0, 0)
-    for i in range(4):
-        enc[0, pl.ds(i * 128, 128)] = finish(0, i, first[0, i])
+        pl.semaphore_wait(know.at[4], NH - 1)
 
     with scope("wait_rows"):
-        for s in range(4):
-            for i in range(NH - 1):
-                row_copy(i, s).wait_recv()
+        for i in range(NH - 1):
+            all_rows(i, rr_sem).wait()
 
     for chip in range(4):
         to_x = lax.rem(lax.div(h, 2) + STEPS[2 * chip][0], 4)
         rows = pl.ds(pl.multiple_of(to_x * 512, 512), 512)
         with scope("terms"):
-            total = placed[rows] + jnp.dot(place[0, rows], enc[0], preferred_element_type=F32)
+            total = placed[rows] + jnp.dot(
+                place[rows, :512], enc[:512], preferred_element_type=F32
+            )
             pair = rbuf[pl.ds(to_x * 2, 2)].reshape(512, C)
             tsend[rows] = (pair.astype(F32) - total).astype(BF16)
 
@@ -514,32 +580,41 @@
         gr_sem.at[3],
     ).start()
 
+    with scope("spread"):
+        make_spread()
+
     with scope("grad"):
         up_in.wait()
         rows_all = rbuf[...].reshape(SLOTS, C)
         for j in range(8):
             pick = pick_rows(column(slot[pl.ds(j, 1), :].astype(F32)), SLOTS // 128)
             quant = jnp.dot(pick, rows_all, preferred_element_type=F32)
-            cells = pl.ds((j % 4) * 128, 128)
-            grad_out[pl.ds(j * 128, 128)] = rotate_back(
-                enc[j // 4, cells].astype(F32), quant, up[pl.ds(j * 128, 128)].astype(F32)
+            cells = pl.ds(j * 128, 128)
+            grad_out[cells] = rotate_back(
+                enc[cells].astype(F32), quant, up[cells].astype(F32)
             ).astype(BF16)
     grad_done = pltpu.make_async_copy(grad_out, grad_hbm, out_sem.at[0])
     grad_done.start()
 
     for i in range(NH - 1):
         code_copy(i).wait_send()
-        for s in range(4):
-            row_copy(i, s).wait_send()
+        all_rows(i, rs_sem).wait()
     for dt in range(1, NT):
         key_copy(dt).wait_send()
     for c in range(2):
         for e in range(4):
             for d in range(2):
-                x_copy(c, e, d).wait_send()
-        for e in range(2):
-            for part in range(3):
-                t_copy(c, e, part).wait_send()
+                given = gives_x(d) if e > 1 else jnp.logical_and(t > 0, gives_x(d))
+
+                @pl.when(given)
+                def _():
+                    x_copy(c, e, d).wait_send()
+
+        @pl.when(t < NT - 1)
+        def _():
+            for e in range(2):
+                for part in range(3):
+                    t_copy(c, e, part).wait_send()
 
     def arrived(chip):
         part = pl.ds(chip * 512, 512)
@@ -549,30 +624,29 @@
     def summed(rows, part):
         return jnp.dot(spread_in[rows, part], trecv[part], preferred_element_type=F32)
 
-    everything = pl.ds(0, K_OWN)
     arrived(0)
-    arrived(1)
     with scope("sums"):
-        sums[...] = summed(everything, pl.ds(0, 1024))
-    arrived(2)
-    with scope("sums"):
-        sums[...] += summed(everything, pl.ds(1024, 512))
+        for b in range(4):
+            rows = pl.ds(b * 512, 512)
+            sums[rows] = summed(rows, pl.ds(0, 512))
     sent = pl.ds(0, SLOTS - CAP)
     with scope("sent"):
         pltpu.make_async_copy(tsend.at[sent], tsend.at[sent], gs_sem).wait()
-    arrived(3)
+    for chip in range(1, 4):
+        arrived(chip)
     done = []
     with scope("sums"):
         for b in range(2):
             rows = pl.ds(b * 1024, 1024)
-            total = sums[rows] + summed(rows, pl.ds(1536, 512))
+            total = sums[rows] + summed(rows, pl.ds(512, 1536))
             sums_out[rows] = (2.0 * total).astype(BF16)
             copy = pltpu.make_async_copy(sums_out.at[rows], sums_hbm.at[rows], out_sem.at[1 + b])
             copy.start()
             done.append(copy)
-    grad_done.wait()
-    for copy in done:
-        copy.wait()
+    with scope("out"):
+        grad_done.wait()
+        for copy in done:
+            copy.wait()
 
 
 def window(latents, w1, w2, book, codes, upstream):
@@ -595,14 +669,14 @@
             pltpu.VMEM((4, 512, 3 * C), BF16),
             pltpu.VMEM((2, 512, 3 * C), F32),
             pltpu.VMEM((2, 4, 128, C), BF16),
-            pltpu.VMEM((2, 512, C), BF16),
+            pltpu.VMEM((CELLS, C), BF16),
             pltpu.VMEM((OWN, 128), I32),
             pltpu.VMEM((8, 128), I32),
             pltpu.VMEM((NT, NH, 128), I32),
-            pltpu.VMEM((4, K_OWN, C), BF16),
+            pltpu.VMEM((8, K_OWN, C), BF16),
             pltpu.VMEM((NH, 256, C), BF16),
             pltpu.VMEM((NH, 256, C), BF16),
-            pltpu.VMEM((2, SLOTS, 512), BF16),
+            pltpu.VMEM((SLOTS, CELLS), BF16),
             pltpu.VMEM((SLOTS, C), F32),
             pltpu.VMEM((SLOTS, C), BF16),
             pltpu.VMEM((SLOTS, C), BF16),
@@ -619,15 +693,15 @@
             dma((2, 2, 3)),
             dma((NH,)),
             dma((NH,)),
-            dma((4,)),
-            dma((NH, 4)),
-            dma((NH, 4)),
+            dma((8,)),
+            dma((NH,)),
+            dma((NH,)),
             dma((NT,)),
             dma((NT,)),
             dma,
             dma((4,)),
             dma((3,)),
-            pltpu.SemaphoreType.REGULAR((4,)),
+            pltpu.SemaphoreType.REGULAR((5,)),
         ],
         compiler_params=pltpu.CompilerParams(
             collective_id=0, has_side_effects=True, vmem_limit_bytes=VMEM_LIMIT

time: 63.7 us -> 58.1 us (0.912)
  Pallas kernels: 62.7 us -> 56.9 us
    pallas_call x1, Pallas kernels: 60.5 us -> 54.7 us  [window(): pl.pallas_call(window_kernel, out_shape=(jax.ShapeDtypeStruct((CELLS, C),...]
where the time goes in v4:
time: 58.1 us; the launch traced here: 57.7 us
  Pallas kernels  56.9 us (98%)
  between operations  0.8 us (1%)
    pallas_call x1, Pallas kernels, window(): pl.pallas_call(window_kernel, out_shape=(jax.ShapeDtypeStruct((CELLS, C),...  54.7 us
    pallas_call x1, Pallas kernels, hand_over(): pl.pallas_call(hand_kernel, out_shape=(jax.ShapeDtypeStruct((CELLS, C), B...  2.19 us

profile of v4, /device:TPU:1, one launch (start us, length us, event | category | flops | bytes accessed | tf_op | source)
XLA Modules:
  0.0 57.7 jit_solution(8008404938980466865)
XLA Ops:
  0.6 54.7 %window.1 = (bf16[1024,256]{1,0:T(8,128)(2,1)}, bf16[2048,256]{1,0:T(8,128)(2,1)}) custom-call(bf16[2,4,128,256]{3,2,1,0:T(8,128)(2,1)} %lat_hbm.1, bf16[3,3,3,256,256]{4,3,2,1,0:T(8,128)(2,1)} %w1_ref.1, bf16[3,3,3,256,256]{4,3,2,1,0:T(8,128)(2,1)} %w2_ref.1, bf16[32768,256]{1,0:T(8,128)(2,1)} %book_ref.1, s32[8,128]{1,0:T(8,128)} %bitcast.4, ...), custom_call_target="tpu_custom_call" | custom-call | tf_op jit(solution)/shard_map/window/pallas_call | solution.py:656
  55.3 2.2 %hand_over.1 = (bf16[1024,256]{1,0:T(8,128)(2,1)}, bf16[2048,256]{1,0:T(8,128)(2,1)}) custom-call(bf16[1024,256]{1,0:T(8,128)(2,1)} %get-tuple-element.6.grad_in, bf16[2048,256]{1,0:T(8,128)(2,1)} %get-tuple-element.7.sums_in), custom_call_target="tpu_custom_call" | custom-call | tf_op jit(solution)/shard_map/hand_over/pallas_call | solution.py:733

commit v5 on v4

--- a/solution.py
+++ b/solution.py
@@ -61,12 +61,13 @@
     w1_ref,
     w2_ref,
     book_ref,
-    codes_ref,
+    codes_hbm,
     up_hbm,
     grad_hbm,
     sums_hbm,
     lat,
     up,
+    codes_ref,
     wv,
     ext,
     cat,
@@ -113,6 +114,13 @@
     def at_h(by):
         return lax.rem(h + by, NH)
 
+    lat_in = [pltpu.make_async_copy(lat_hbm.at[f], lat.at[f], in_sem.at[f]) for f in range(2)]
+    up_in = pltpu.make_async_copy(up_hbm, up, in_sem.at[2])
+    codes_in = pltpu.make_async_copy(codes_hbm, codes_ref, in_sem.at[3])
+    lat_in[1].start()
+    codes_in.start()
+    lat_in[0].start()
+
     barrier = pltpu.get_barrier_semaphore()
 
     def if_in(by):
@@ -132,11 +140,6 @@
 
     def all_entered():
         pl.semaphore_wait(barrier, NH - 1 + places(1))
-
-    lat_in = [pltpu.make_async_copy(lat_hbm.at[f], lat.at[f], in_sem.at[f]) for f in range(2)]
-    up_in = pltpu.make_async_copy(up_hbm, up, in_sem.at[2])
-    lat_in[1].start()
-    lat_in[0].start()
 
     def weights_start(c, p):
         w_ref = (w1_ref, w2_ref)[c]
@@ -161,7 +164,7 @@
         return pltpu.make_async_remote_copy(
             src_ref=ext.at[c, e, src],
             dst_ref=ext.at[c, e, dst],
-            send_sem=xs_sem.at[c, e, d],
+            send_sem=xs_sem.at[d if e > 1 else 2 + d],
             recv_sem=xr_sem.at[c, e, d],
             device_id=(t, to),
             device_id_type=MESH,
@@ -172,7 +175,7 @@
         return pltpu.make_async_remote_copy(
             src_ref=ext.at[c, e + 2, rows],
             dst_ref=ext.at[c, e, rows],
-            send_sem=ts_sem.at[c, e, part],
+            send_sem=ts_sem,
             recv_sem=tr_sem.at[c, e, part],
             device_id=(lax.rem(t + 1, NT), h),
             device_id_type=MESH,
@@ -206,8 +209,8 @@
         return pltpu.make_async_remote_copy(
             src_ref=msg.at[pl.ds(pl.multiple_of(to * NT, NT), NT)],
             dst_ref=rcodes.at[:, h],
-            send_sem=cs_sem.at[i],
-            recv_sem=cr_sem.at[i],
+            send_sem=cs_sem,
+            recv_sem=cr_sem,
             device_id=(t, to),
             device_id_type=MESH,
         )
@@ -217,8 +220,8 @@
         return pltpu.make_async_remote_copy(
             src_ref=sbuf.at[to, pl.ds(g * CAP, CAP)],
             dst_ref=rbuf.at[h, pl.ds(g * CAP, CAP)],
-            send_sem=rs_sem.at[i],
-            recv_sem=rr_sem.at[i],
+            send_sem=rs_sem,
+            recv_sem=rr_sem,
             device_id=(t, to),
             device_id_type=MESH,
         )
@@ -228,8 +231,8 @@
         return pltpu.make_async_remote_copy(
             src_ref=rcodes.at[to],
             dst_ref=crecv.at[:, t],
-            send_sem=ks_sem.at[dt],
-            recv_sem=kr_sem.at[dt],
+            send_sem=ks_sem,
+            recv_sem=kr_sem,
             device_id=(to, h),
             device_id_type=MESH,
         )
@@ -355,8 +358,8 @@
             for i in range(NH - 1):
                 row_copy(i, g).start()
 
-    def all_rows(i, sem):
-        return pltpu.make_async_copy(rbuf.at[i], rbuf.at[i], sem.at[i])
+    def bytes_of(ref, sem):
+        pltpu.make_async_copy(ref, ref, sem).wait()
 
     def tell(r):
         for by in (2**r, -(2**r)):
@@ -381,9 +384,7 @@
             lay_one_hot(place, pl.ds(j * 128, 128), slot[pl.ds(j, 1), :])
 
     def make_spread():
-        for dt in range(1, NT):
-            key_copy(dt).wait_recv()
-        own_keys.wait()
+        bytes_of(crecv, kr_sem)
         for i in range(NH):
             keys = crecv[column_at(i, -1)]
             for half in range(2):
@@ -429,8 +430,6 @@
         with scope("gather"):
             gather(k)
 
-    with scope("slots"):
-        make_slots()
     for f in (1, 0):
         with scope("latin"):
             lat_in[f].wait()
@@ -438,14 +437,17 @@
             for i in range(4):
                 ext[0, 2 + f, 1 + i] = norm_act(lat[f, i].astype(F32))
         if f == 1:
-            weights_start(0, 2)
             with scope("barrier"):
                 all_entered()
         send_frame(0, f)
         if f == 1:
+            tell(0)
+            with scope("slots"):
+                codes_in.wait()
+                make_slots()
             for i in range(NH - 1):
                 code_copy(i).start()
-    tell(0)
+    weights_start(0, 2)
     for g in range(4):
         book_copy(g).start()
     weights_start(0, 1)
@@ -455,14 +457,13 @@
         book_copy(g).start()
     with scope("place"):
         make_place()
-    with scope("asked"):
-        for i in range(NH - 1):
-            code_copy(i).wait_recv()
-    fetch(0)
-    send_rows(0, 1)
     rows_of(0, 3)
     weights_here(0, 2)
     mm(1, 0, 3, 2, fresh=True)
+    with scope("asked"):
+        bytes_of(msg.at[pl.ds(0, OWN - NT)], cr_sem)
+    fetch(0)
+    send_rows(0, 1)
     rows_of(0, 2)
     forward(0, 1)
     send_rows(2)
@@ -470,72 +471,70 @@
     mm(1, 0, 2, 1)
     send_rows(3)
     mm(0, 0, 2, 2, fresh=True)
+    fetch(1)
+    send_rows(4)
+    with scope("know"):
+        told(0)
+    tell(1)
     for p in (2, 1, 0):
         weights_start(1, p)
+    fetch(2)
     earlier_frame(0, 1)
+    forward(0, 0)
+    send_rows(5, 6)
     weights_here(0, 0)
     with scope("widen"):
         widen(0, 1)
     mm(1, 0, 1, 0)
     next_frame(1)
-    fetch(1)
-    forward(0, 0)
-    send_rows(4)
+    send_rows(7)
     mm(0, 0, 1, 1)
-    send_rows(5)
     with scope("know"):
-        told(0)
-    tell(1)
-    fetch(2)
-    send_rows(6)
+        told(1)
+    tell(2)
+    send_rows(8)
+    fetch(3)
+    rbuf[h] = sbuf[h]
+    up_in.start()
     earlier_frame(0, 0)
-    send_rows(7)
+    send_rows(9)
     with scope("widen"):
         widen(0, 0)
     mm(0, 0, 0, 0)
     next_frame(0)
-    send_rows(8)
-    with scope("know"):
-        told(1)
-    tell(2)
-    rows_of(1, 3)
-    weights_here(1, 2)
-    mm(1, 1, 3, 2, fresh=True)
     forward(1, 1)
-    send_rows(9)
-    fetch(3)
-    rbuf[h] = sbuf[h]
-    up_in.start()
     send_rows(10)
     with scope("know"):
         told(2)
     tell(3)
+    rows_of(1, 3)
+    send_rows(11)
+    weights_here(1, 2)
+    mm(1, 1, 3, 2, fresh=True)
+    send_rows(12)
     rows_of(1, 2)
-    send_rows(11)
+    send_rows(13)
     weights_here(1, 1)
     mm(1, 1, 2, 1)
-    send_rows(12)
+    send_rows(14)
     mm(0, 1, 2, 2, fresh=True)
-    earlier_frame(1, 1)
-    send_rows(13)
-    weights_here(1, 0)
-    with scope("widen"):
-        widen(1, 1)
-    mm(1, 1, 1, 0)
-    send_rows(14)
-    for i in range(4):
-        enc[pl.ds(512 + i * 128, 128)] = finish(1, i, first[1, i])
-    mm(0, 1, 1, 1)
-    forward(1, 0)
     send_rows(15)
     with scope("know"):
         told(3)
     for i in range(1, NH):
         pl.semaphore_signal(know.at[4], inc=1, device_id=(t, at_h(i)), device_id_type=MESH)
+    earlier_frame(1, 1)
+    forward(1, 0)
+    weights_here(1, 0)
+    with scope("widen"):
+        widen(1, 1)
+    mm(1, 1, 1, 0)
+    for i in range(4):
+        enc[pl.ds(512 + i * 128, 128)] = finish(1, i, first[1, i])
+    mm(0, 1, 1, 1)
     for dt in range(1, NT):
         key_copy(dt).start()
-    own_keys = pltpu.make_async_copy(rcodes.at[t], crecv.at[:, t], kr_sem.at[0])
-    own_keys.start()
+    pltpu.make_async_copy(rcodes.at[t], crecv.at[:, t], kr_sem).start()
     with scope("placed"):
         for b in range(4):
             rows = pl.ds(b * 512, 512)
@@ -550,8 +549,7 @@
         pl.semaphore_wait(know.at[4], NH - 1)
 
     with scope("wait_rows"):
-        for i in range(NH - 1):
-            all_rows(i, rr_sem).wait()
+        bytes_of(rbuf.at[pl.ds(0, NH - 1)], rr_sem)
 
     for chip in range(4):
         to_x = lax.rem(lax.div(h, 2) + STEPS[2 * chip][0], 4)
@@ -596,25 +594,22 @@
     grad_done = pltpu.make_async_copy(grad_out, grad_hbm, out_sem.at[0])
     grad_done.start()
 
-    for i in range(NH - 1):
-        code_copy(i).wait_send()
-        all_rows(i, rs_sem).wait()
-    for dt in range(1, NT):
-        key_copy(dt).wait_send()
-    for c in range(2):
-        for e in range(4):
-            for d in range(2):
-                given = gives_x(d) if e > 1 else jnp.logical_and(t > 0, gives_x(d))
-
-                @pl.when(given)
-                def _():
-                    x_copy(c, e, d).wait_send()
-
-        @pl.when(t < NT - 1)
+    bytes_of(msg.at[pl.ds(0, OWN - NT)], cs_sem)
+    bytes_of(rbuf.at[pl.ds(0, NH - 1)], rs_sem)
+    bytes_of(rcodes.at[pl.ds(0, NT - 1)], ks_sem)
+    for d in range(2):
+
+        @pl.when(gives_x(d))
         def _():
-            for e in range(2):
-                for part in range(3):
-                    t_copy(c, e, part).wait_send()
+            bytes_of(ext.at[0, 0, pl.ds(0, 4)], xs_sem.at[d])
+
+        @pl.when(jnp.logical_and(t > 0, gives_x(d)))
+        def _():
+            bytes_of(ext.at[0, 0, pl.ds(0, 4)], xs_sem.at[2 + d])
+
+    @pl.when(t < NT - 1)
+    def _():
+        bytes_of(rbuf, ts_sem)
 
     def arrived(chip):
         part = pl.ds(chip * 512, 512)
@@ -632,17 +627,26 @@
     sent = pl.ds(0, SLOTS - CAP)
     with scope("sent"):
         pltpu.make_async_copy(tsend.at[sent], tsend.at[sent], gs_sem).wait()
-    for chip in range(1, 4):
-        arrived(chip)
+    arrived(1)
+    with scope("sums"):
+        for b in range(4):
+            rows = pl.ds(b * 512, 512)
+            sums[rows] += summed(rows, pl.ds(512, 512))
+    arrived(2)
+    arrived(3)
     done = []
     with scope("sums"):
         for b in range(2):
             rows = pl.ds(b * 1024, 1024)
-            total = sums[rows] + summed(rows, pl.ds(512, 1536))
+            total = sums[rows] + summed(rows, pl.ds(1024, 1024))
             sums_out[rows] = (2.0 * total).astype(BF16)
-            copy = pltpu.make_async_copy(sums_out.at[rows], sums_hbm.at[rows], out_sem.at[1 + b])
-            copy.start()
-            done.append(copy)
+            for n in range(2):
+                rows = pl.ds(b * 1024 + n * 512, 512)
+                copy = pltpu.make_async_copy(
+                    sums_out.at[rows], sums_hbm.at[rows], out_sem.at[1 + 2 * b + n]
+                )
+                copy.start()
+                done.append(copy)
     with scope("out"):
         grad_done.wait()
         for copy in done:
@@ -650,7 +654,6 @@
 
 
 def window(latents, w1, w2, book, codes, upstream):
-    vm = pl.BlockSpec(memory_space=pltpu.VMEM)
     hbm = pl.BlockSpec(memory_space=pl.ANY)
     dma = pltpu.SemaphoreType.DMA
     return pl.pallas_call(
@@ -659,11 +662,12 @@
             jax.ShapeDtypeStruct((CELLS, C), BF16),
             jax.ShapeDtypeStruct((K_OWN, C), BF16),
         ),
-        in_specs=[hbm, hbm, hbm, hbm, vm, hbm],
+        in_specs=[hbm] * 6,
         out_specs=(hbm, hbm),
         scratch_shapes=[
             pltpu.VMEM((2, 4, 128, C), BF16),
             pltpu.VMEM((CELLS, C), BF16),
+            pltpu.VMEM((8, 128), I32),
             pltpu.VMEM((2, 3, 3 * C, 3 * C), BF16),
             pltpu.VMEM((2, 4, 6, 128, C), BF16),
             pltpu.VMEM((4, 512, 3 * C), BF16),
@@ -685,22 +689,22 @@
             pltpu.VMEM((K_OWN, C), F32),
             pltpu.VMEM((K_OWN, C), BF16),
             pltpu.VMEM((CELLS, C), BF16),
-            dma((3,)),
+            dma((4,)),
             dma((2, 3)),
+            dma((4,)),
             dma((2, 4, 2)),
-            dma((2, 4, 2)),
+            dma,
             dma((2, 2, 3)),
-            dma((2, 2, 3)),
-            dma((NH,)),
-            dma((NH,)),
+            dma,
+            dma,
             dma((8,)),
-            dma((NH,)),
-            dma((NH,)),
-            dma((NT,)),
-            dma((NT,)),
+            dma,
+            dma,
+            dma,
+            dma,
             dma,
             dma((4,)),
-            dma((3,)),
+            dma((5,)),
             pltpu.SemaphoreType.REGULAR((5,)),
         ],
         compiler_params=pltpu.CompilerParams(
@@ -711,7 +715,7 @@
 
 
 def hand_kernel(grad_in, sums_in, grad_ref, sums_ref, grad_buf, sums_buf, in_sem, out_sem):
-    pieces = [(grad_in, grad_buf, grad_ref, 0), (grad_in, grad_buf, grad_ref, 1)] + [
+    pieces = [(grad_in, grad_buf, grad_ref, k) for k in range(2)] + [
         (sums_in, sums_buf, sums_ref, k) for k in range(4)
     ]
     ins, outs = [], []

time: 58.1 us -> 55 us (0.947)
  Pallas kernels: 56.9 us -> 54.1 us
    pallas_call x1, Pallas kernels: 54.7 us -> 51.9 us  [window(): pl.pallas_call(window_kernel, out_shape=(jax.ShapeDtypeStruct((CELLS, C),...]
where the time goes in v5:
time: 55 us; the launch traced here: 54.9 us
  Pallas kernels  54.1 us (98%)
  between operations  0.8 us (1%)
    pallas_call x1, Pallas kernels, window(): pl.pallas_call(window_kernel, out_shape=(jax.ShapeDtypeStruct((CELLS, C),...  51.9 us
    pallas_call x1, Pallas kernels, hand_over(): pl.pallas_call(hand_kernel, out_shape=(jax.ShapeDtypeStruct((CELLS, C), B...  2.19 us

profile of v5, /device:TPU:1, one launch (start us, length us, event | category | flops | bytes accessed | tf_op | source)
XLA Modules:
  0.0 54.9 jit_solution(9204955794378458131)
XLA Ops:
  0.6 51.9 %window.1 = (bf16[1024,256]{1,0:T(8,128)(2,1)}, bf16[2048,256]{1,0:T(8,128)(2,1)}) custom-call(bf16[2,4,128,256]{3,2,1,0:T(8,128)(2,1)} %lat_hbm.1, bf16[3,3,3,256,256]{4,3,2,1,0:T(8,128)(2,1)} %w1_ref.1, bf16[3,3,3,256,256]{4,3,2,1,0:T(8,128)(2,1)} %w2_ref.1, bf16[32768,256]{1,0:T(8,128)(2,1)} %book_ref.1, s32[8,128]{1,0:T(8,128)} %bitcast.4, ...), custom_call_target="tpu_custom_call" | custom-call | tf_op jit(solution)/shard_map/window/pallas_call | solution.py:659
  52.5 2.2 %hand_over.1 = (bf16[1024,256]{1,0:T(8,128)(2,1)}, bf16[2048,256]{1,0:T(8,128)(2,1)}) custom-call(bf16[1024,256]{1,0:T(8,128)(2,1)} %get-tuple-element.6.grad_in, bf16[2048,256]{1,0:T(8,128)(2,1)} %get-tuple-element.7.sums_in), custom_call_target="tpu_custom_call" | custom-call | tf_op jit(solution)/shard_map/hand_over/pallas_call | solution.py:737

commit v6 on v5

--- a/solution.py
+++ b/solution.py
@@ -480,12 +480,12 @@
         weights_start(1, p)
     fetch(2)
     earlier_frame(0, 1)
-    forward(0, 0)
-    send_rows(5, 6)
     weights_here(0, 0)
     with scope("widen"):
         widen(0, 1)
     mm(1, 0, 1, 0)
+    forward(0, 0)
+    send_rows(5, 6)
     next_frame(1)
     send_rows(7)
     mm(0, 0, 1, 1)
@@ -524,11 +524,11 @@
     for i in range(1, NH):
         pl.semaphore_signal(know.at[4], inc=1, device_id=(t, at_h(i)), device_id_type=MESH)
     earlier_frame(1, 1)
-    forward(1, 0)
     weights_here(1, 0)
     with scope("widen"):
         widen(1, 1)
     mm(1, 1, 1, 0)
+    forward(1, 0)
     for i in range(4):
         enc[pl.ds(512 + i * 128, 128)] = finish(1, i, first[1, i])
     mm(0, 1, 1, 1)

time: 55 us -> 54.9 us (level)
  no operation moved by 1% of the time
where the time goes in v6:
time: 54.9 us; the launch traced here: 54.7 us
  Pallas kernels  53.9 us (98%)
  between operations  0.8 us (1%)
    pallas_call x1, Pallas kernels, window(): pl.pallas_call(window_kernel, out_shape=(jax.ShapeDtypeStruct((CELLS, C),...  51.7 us
    pallas_call x1, Pallas kernels, hand_over(): pl.pallas_call(hand_kernel, out_shape=(jax.ShapeDtypeStruct((CELLS, C), B...  2.19 us

profile of v6, /device:TPU:1, one launch (start us, length us, event | category | flops | bytes accessed | tf_op | source)
XLA Modules:
  0.0 54.7 jit_solution(453080743468600600)
XLA Ops:
  0.6 51.7 %window.1 = (bf16[1024,256]{1,0:T(8,128)(2,1)}, bf16[2048,256]{1,0:T(8,128)(2,1)}) custom-call(bf16[2,4,128,256]{3,2,1,0:T(8,128)(2,1)} %lat_hbm.1, bf16[3,3,3,256,256]{4,3,2,1,0:T(8,128)(2,1)} %w1_ref.1, bf16[3,3,3,256,256]{4,3,2,1,0:T(8,128)(2,1)} %w2_ref.1, bf16[32768,256]{1,0:T(8,128)(2,1)} %book_ref.1, s32[8,128]{1,0:T(8,128)} %bitcast.4, ...), custom_call_target="tpu_custom_call" | custom-call | tf_op jit(solution)/shard_map/window/pallas_call | solution.py:659
  52.4 2.2 %hand_over.1 = (bf16[1024,256]{1,0:T(8,128)(2,1)}, bf16[2048,256]{1,0:T(8,128)(2,1)}) custom-call(bf16[1024,256]{1,0:T(8,128)(2,1)} %get-tuple-element.6.grad_in, bf16[2048,256]{1,0:T(8,128)(2,1)} %get-tuple-element.7.sums_in), custom_call_target="tpu_custom_call" | custom-call | tf_op jit(solution)/shard_map/hand_over/pallas_call | solution.py:737
